TPU v7x, 128 devices: a whole 4x4x4 slice. The times are simulated.
128 devices in a mesh: seq: 16 (over x, y), segment: 8 (over z, core).
Axes of the slice: x: 4, y: 4, z: 4, core: 2. Of those that a mesh axis runs over, the one named last changes fastest.
Arguments:
- base_state: bfloat16 [2048, 1024], P('seq'), may hold values from -6 to 6
- forcing: float32 [2048, 64], P('seq'), may hold values from -6 to 6
- theta_base: float32 [64], replicated, may hold values from -1 to 1
- perturb: float32 [32, 64], replicated, may hold values from -6 to 6
- order: int32 [32], replicated, may hold values from 0 to 31, each once
- w_force: bfloat16 [64, 1024], replicated, may hold values from -0.75 to 0.75
- attn_gain: float32 [8, 1024], P('segment'), may hold values from 0.25 to 1.75
- w_query: bfloat16 [8, 1024, 1024], P('segment'), may hold values from -16 to 16
- w_key: bfloat16 [8, 1024, 1024], P('segment'), may hold values from -1 to 1, as said below
- w_value: bfloat16 [8, 1024, 1024], P('segment'), may hold values from -0.1875 to 0.1875
- w_out: bfloat16 [8, 1024, 1024], P('segment'), may hold values from -0.1875 to 0.1875
- block_mask: int32 [16, 4], P('seq'), may hold values 0 or 1
- out_gain: float32 [1024], replicated, may hold values from 0.25 to 1.75
- w_read: bfloat16 [1024, 128], replicated, may hold values from -0.1875 to 0.1875
- observed: float32 [2048, 128], P('seq'), may hold values from -8 to 8
Outputs:
- predictions: float32 [8, 2048, 128], P('segment', 'seq')
- fitness: float32 [8], P('segment')
Inputs may be any that keep to these rules, and one draw needn't show every extreme that they name: `order`: each pool index appears once. `w_key`: a projection matrix of order one over square root of 1024.
All inputs are finite; a program needn't handle non-finite values. No bound on the sum of `block_mask` on one device may be relied on, other than what follows from the above.
Results may differ from a plain program's by a relative error of at most 0.02.
Values may be sent and summed in bfloat16 or wider, within the bound.
A program may use at most 64 MiB of HBM per device.

v0:
```python
import jax
import jax.numpy as jnp
from jax import lax
from jax.sharding import PartitionSpec as P

HEADS = 16
LEVELS = 4


def from_behind(value, axis, steps):
    count = lax.axis_size(axis)
    leading, last = (max(0, -steps), min(count, count - steps))
    return lax.ppermute(value, axis, [(source, source + steps) for source in range(leading, last)])


def from_root(value, axis, root):
    mine = lax.axis_index(axis) == root
    return lax.psum(jnp.where(mine, value, jnp.zeros_like(value)), axis)


def norm_rows(state, gain):
    values = state.astype(jnp.float32)
    meansq = jnp.mean(values * values, axis=-1, keepdims=True) + 1e-05
    return (values * lax.rsqrt(meansq) * gain).astype(jnp.bfloat16)


def attend(queries, keys_all, values_all, visible):
    rows = queries.shape[0]
    count = keys_all.shape[0]
    qhead = queries.reshape(rows, HEADS, -1)
    khead = keys_all.reshape(count, HEADS, -1)
    vhead = values_all.reshape(count, HEADS, -1)
    scores = jnp.einsum("qhe,khe->hqk", qhead, khead, preferred_element_type=jnp.float32) * 0.125
    scores = jnp.where(visible[None], scores, -1e30)
    peak = jnp.max(scores, axis=-1, keepdims=True)
    expon = jnp.exp(scores - peak)
    weights = (expon / jnp.sum(expon, axis=-1, keepdims=True)).astype(jnp.bfloat16)
    context = jnp.einsum("hqk,khe->qhe", weights, vhead, preferred_element_type=jnp.float32)
    return context.reshape(rows, -1).astype(jnp.bfloat16)


def section(state, gain, wq, wk, wv, wo, mask_row):
    rows = state.shape[0]
    normed = norm_rows(state, gain)
    queries = jnp.dot(normed, wq, preferred_element_type=jnp.float32).astype(jnp.bfloat16)
    keys_loc = jnp.dot(normed, wk, preferred_element_type=jnp.float32).astype(jnp.bfloat16)
    values_loc = jnp.dot(normed, wv, preferred_element_type=jnp.float32).astype(jnp.bfloat16)
    here = lax.axis_index("seq")
    causal = jnp.arange(rows)[:, None] >= jnp.arange(rows)[None, :]
    key_parts = [keys_loc]
    value_parts = [values_loc]
    visible_parts = [causal]
    outgoing = jnp.stack([keys_loc, values_loc])
    for level in range(LEVELS):
        offset = 2**level
        arrived = from_behind(outgoing, "seq", offset)
        key_parts.append(arrived[0])
        value_parts.append(arrived[1])
        usable = (mask_row[level] == 1) & (here >= offset)
        visible_parts.append(jnp.broadcast_to(usable, (rows, rows)))
    keys_all = jnp.concatenate(key_parts, axis=0)
    values_all = jnp.concatenate(value_parts, axis=0)
    visible = jnp.concatenate(visible_parts, axis=1)
    context = attend(queries, keys_all, values_all, visible)
    mixed = state.astype(jnp.float32) + jnp.dot(context, wo, preferred_element_type=jnp.float32)
    return mixed.astype(jnp.bfloat16)


def per_device(
    base_state,
    forcing,
    theta_base,
    perturb,
    order,
    w_force,
    attn_gain,
    w_query,
    w_key,
    w_value,
    w_out,
    block_mask,
    out_gain,
    w_read,
    observed,
):
    segment_now = lax.axis_index("segment")
    segments = lax.axis_size("segment")
    pool_size = perturb.shape[0]
    rows, width = base_state.shape
    channels = observed.shape[1]
    selector = (order[:segments][:, None] == jnp.arange(pool_size)[None, :]).astype(jnp.float32)
    theta = theta_base[None, :] + 0.5 * jnp.dot(selector, perturb, precision=lax.Precision.HIGHEST)
    drive = forcing[None, :, :] * theta[:, None, :]
    lifted = jnp.einsum(
        "mtp,pd->mtd", drive, w_force.astype(jnp.float32), precision=lax.Precision.HIGHEST
    )
    starts = (base_state.astype(jnp.float32)[None] + lifted).astype(jnp.bfloat16)
    gain = attn_gain[0]
    mask_row = block_mask[0]

    def advance(count, carry):
        carried, stored = carry
        entry = lax.dynamic_index_in_dim(
            starts, jnp.minimum(count, segments - 1), 0, keepdims=False
        )
        current = jnp.where(segment_now == 0, entry, carried)
        result = section(current, gain, w_query[0], w_key[0], w_value[0], w_out[0], mask_row)
        slot = count - segment_now
        predicted = jnp.dot(norm_rows(result, out_gain), w_read, preferred_element_type=jnp.float32)
        finished = (segment_now == segments - 1) & (slot >= 0) & (slot < segments)
        updated = lax.dynamic_update_index_in_dim(
            stored, predicted, jnp.clip(slot, 0, segments - 1), 0
        )
        stored = jnp.where(finished, updated, stored)
        carried = from_behind(result, "segment", 1)
        return (carried, stored)

    initial = (
        jnp.zeros((rows, width), jnp.bfloat16),
        jnp.zeros((segments, rows, channels), jnp.float32),
    )
    carried, stored = lax.fori_loop(0, segments + segments - 1, advance, initial)
    everything = from_root(stored.astype(jnp.bfloat16), "segment", segments - 1).astype(
        stored.dtype
    )
    mine = lax.dynamic_index_in_dim(everything, segment_now, 0, keepdims=False)
    length = rows * lax.axis_size("seq")
    hours = (lax.axis_index("seq") * rows + jnp.arange(rows)).astype(jnp.float32)
    hour_weight = 1.0 + 2.0 * hours / (length - 1)
    errors = mine - observed
    partial_sum = jnp.sum(hour_weight[:, None] * errors * errors)
    total = lax.psum(partial_sum, "seq")
    fitness = -total / (length * channels)
    return (mine[None], jnp.reshape(fitness, (1,)))


def solution(mesh):
    placed = (
        P("seq", None),
        P("seq", None),
        P(),
        P(),
        P(),
        P(),
        P("segment", None),
        P("segment", None, None),
        P("segment", None, None),
        P("segment", None, None),
        P("segment", None, None),
        P("seq", None),
        P(),
        P(),
        P("seq", None),
    )
    return jax.shard_map(
        per_device,
        mesh=mesh,
        in_specs=placed,
        out_specs=(P("segment", "seq", None), P("segment")),
        check_vma=False,
    )
```

profile of v0, /device:TPU:64, one launch (start us, length us, event | category | flops | bytes accessed | tf_op | source)
XLA Modules:
  0.0 1393.2 jit_solution(11179896485285453180)
XLA Ops:
  18.4 1239.9 %while.17 = (s32[]{:T(128)}, bf16[128,1024]{1,0:T(8,128)(2,1)S(1)}, bf16[8,128,128]{2,1,0:T(8,128)(2,1)}, pred[]{:T(512)}, bf16[8,128,1024]{2,1,0:T(8,128)(2,1)}...) while((s32[]{:T(128)}, bf16[128,1024]{1,0:T(8,128)(2,1)S(1)}, ...), condition=%wide.region_5.6_spmd, body=%wide.region_0.5_spmd.sunk | while | flops 1454932864 | bytes 84481944 | solution.py:122
  25.8 4.8 collective-permute-start.1
  34.1 4.6 collective-permute-start.3
  70.0 5.6 fusion.116
  94.4 27.2 %collective-permute-start.1 = (bf16[2,128,1024]{2,1,0:T(8,128)(2,1)}, bf16[2,128,1024]{2,1,0:T(8,128)(2,1)}, u32[]{:S(2)}, u32[]{:S(2)}) collective-permute-start(bf16[2,128,1024]{2,1,0:T(8,128)(2,1)} %pad_maximum_fusion.2), channel_id=1, source_target_pairs={{0,16},{8,24},{16,32},{24,40},{32,48},{40,56},{48,64},{56,72},{64,... | collective-permute-start | bytes 1572872 | tf_op jit(solution)/shard_map/while/body/eval_jaxpr/ppermute | solution.py:13
  123.7 5.8 collective-permute-start.3
  159.3 5.6 fusion.116
  183.0 28.3 %collective-permute-start.1 = (bf16[2,128,1024]{2,1,0:T(8,128)(2,1)}, bf16[2,128,1024]{2,1,0:T(8,128)(2,1)}, u32[]{:S(2)}, u32[]{:S(2)}) collective-permute-start(bf16[2,128,1024]{2,1,0:T(8,128)(2,1)} %pad_maximum_fusion.2), channel_id=1, source_target_pairs={{0,16},{8,24},{16,32},{24,40},{32,48},{40,56},{48,64},{56,72},{64,... | collective-permute-start | bytes 1572872 | tf_op jit(solution)/shard_map/while/body/eval_jaxpr/ppermute | solution.py:13
  213.4 5.7 collective-permute-start.3
  245.9 5.6 fusion.116
  269.5 27.5 %collective-permute-start.1 = (bf16[2,128,1024]{2,1,0:T(8,128)(2,1)}, bf16[2,128,1024]{2,1,0:T(8,128)(2,1)}, u32[]{:S(2)}, u32[]{:S(2)}) collective-permute-start(bf16[2,128,1024]{2,1,0:T(8,128)(2,1)} %pad_maximum_fusion.2), channel_id=1, source_target_pairs={{0,16},{8,24},{16,32},{24,40},{32,48},{40,56},{48,64},{56,72},{64,... | collective-permute-start | bytes 1572872 | tf_op jit(solution)/shard_map/while/body/eval_jaxpr/ppermute | solution.py:13
  299.1 5.7 collective-permute-start.3
  330.2 5.6 fusion.116
  353.5 23.7 %collective-permute-start.1 = (bf16[2,128,1024]{2,1,0:T(8,128)(2,1)}, bf16[2,128,1024]{2,1,0:T(8,128)(2,1)}, u32[]{:S(2)}, u32[]{:S(2)}) collective-permute-start(bf16[2,128,1024]{2,1,0:T(8,128)(2,1)} %pad_maximum_fusion.2), channel_id=1, source_target_pairs={{0,16},{8,24},{16,32},{24,40},{32,48},{40,56},{48,64},{56,72},{64,... | collective-permute-start | bytes 1572872 | tf_op jit(solution)/shard_map/while/body/eval_jaxpr/ppermute | solution.py:13
  379.3 5.7 collective-permute-start.3
  411.0 5.6 fusion.116
  434.5 25.7 %collective-permute-start.1 = (bf16[2,128,1024]{2,1,0:T(8,128)(2,1)}, bf16[2,128,1024]{2,1,0:T(8,128)(2,1)}, u32[]{:S(2)}, u32[]{:S(2)}) collective-permute-start(bf16[2,128,1024]{2,1,0:T(8,128)(2,1)} %pad_maximum_fusion.2), channel_id=1, source_target_pairs={{0,16},{8,24},{16,32},{24,40},{32,48},{40,56},{48,64},{56,72},{64,... | collective-permute-start | bytes 1572872 | tf_op jit(solution)/shard_map/while/body/eval_jaxpr/ppermute | solution.py:13
  462.3 5.7 collective-permute-start.3
  493.7 5.6 fusion.116
  517.3 25.8 %collective-permute-start.1 = (bf16[2,128,1024]{2,1,0:T(8,128)(2,1)}, bf16[2,128,1024]{2,1,0:T(8,128)(2,1)}, u32[]{:S(2)}, u32[]{:S(2)}) collective-permute-start(bf16[2,128,1024]{2,1,0:T(8,128)(2,1)} %pad_maximum_fusion.2), channel_id=1, source_target_pairs={{0,16},{8,24},{16,32},{24,40},{32,48},{40,56},{48,64},{56,72},{64,... | collective-permute-start | bytes 1572872 | tf_op jit(solution)/shard_map/while/body/eval_jaxpr/ppermute | solution.py:13
  545.3 5.7 collective-permute-start.3
  576.4 5.6 fusion.116
  600.3 25.8 %collective-permute-start.1 = (bf16[2,128,1024]{2,1,0:T(8,128)(2,1)}, bf16[2,128,1024]{2,1,0:T(8,128)(2,1)}, u32[]{:S(2)}, u32[]{:S(2)}) collective-permute-start(bf16[2,128,1024]{2,1,0:T(8,128)(2,1)} %pad_maximum_fusion.2), channel_id=1, source_target_pairs={{0,16},{8,24},{16,32},{24,40},{32,48},{40,56},{48,64},{56,72},{64,... | collective-permute-start | bytes 1572872 | tf_op jit(solution)/shard_map/while/body/eval_jaxpr/ppermute | solution.py:13
  628.3 5.7 collective-permute-start.3
  659.4 5.6 fusion.116
  683.3 25.8 %collective-permute-start.1 = (bf16[2,128,1024]{2,1,0:T(8,128)(2,1)}, bf16[2,128,1024]{2,1,0:T(8,128)(2,1)}, u32[]{:S(2)}, u32[]{:S(2)}) collective-permute-start(bf16[2,128,1024]{2,1,0:T(8,128)(2,1)} %pad_maximum_fusion.2), channel_id=1, source_target_pairs={{0,16},{8,24},{16,32},{24,40},{32,48},{40,56},{48,64},{56,72},{64,... | collective-permute-start | bytes 1572872 | tf_op jit(solution)/shard_map/while/body/eval_jaxpr/ppermute | solution.py:13
  711.2 5.7 collective-permute-start.3
  742.4 5.6 fusion.116
  766.3 25.8 %collective-permute-start.1 = (bf16[2,128,1024]{2,1,0:T(8,128)(2,1)}, bf16[2,128,1024]{2,1,0:T(8,128)(2,1)}, u32[]{:S(2)}, u32[]{:S(2)}) collective-permute-start(bf16[2,128,1024]{2,1,0:T(8,128)(2,1)} %pad_maximum_fusion.2), channel_id=1, source_target_pairs={{0,16},{8,24},{16,32},{24,40},{32,48},{40,56},{48,64},{56,72},{64,... | collective-permute-start | bytes 1572872 | tf_op jit(solution)/shard_map/while/body/eval_jaxpr/ppermute | solution.py:13
  794.2 5.7 collective-permute-start.3
  825.3 5.6 fusion.116
  849.2 25.8 %collective-permute-start.1 = (bf16[2,128,1024]{2,1,0:T(8,128)(2,1)}, bf16[2,128,1024]{2,1,0:T(8,128)(2,1)}, u32[]{:S(2)}, u32[]{:S(2)}) collective-permute-start(bf16[2,128,1024]{2,1,0:T(8,128)(2,1)} %pad_maximum_fusion.2), channel_id=1, source_target_pairs={{0,16},{8,24},{16,32},{24,40},{32,48},{40,56},{48,64},{56,72},{64,... | collective-permute-start | bytes 1572872 | tf_op jit(solution)/shard_map/while/body/eval_jaxpr/ppermute | solution.py:13
  877.2 5.7 collective-permute-start.3
  908.3 5.6 fusion.116
  932.2 25.8 %collective-permute-start.1 = (bf16[2,128,1024]{2,1,0:T(8,128)(2,1)}, bf16[2,128,1024]{2,1,0:T(8,128)(2,1)}, u32[]{:S(2)}, u32[]{:S(2)}) collective-permute-start(bf16[2,128,1024]{2,1,0:T(8,128)(2,1)} %pad_maximum_fusion.2), channel_id=1, source_target_pairs={{0,16},{8,24},{16,32},{24,40},{32,48},{40,56},{48,64},{56,72},{64,... | collective-permute-start | bytes 1572872 | tf_op jit(solution)/shard_map/while/body/eval_jaxpr/ppermute | solution.py:13
  960.1 5.7 collective-permute-start.3
  991.3 5.6 fusion.116
  1015.2 25.8 %collective-permute-start.1 = (bf16[2,128,1024]{2,1,0:T(8,128)(2,1)}, bf16[2,128,1024]{2,1,0:T(8,128)(2,1)}, u32[]{:S(2)}, u32[]{:S(2)}) collective-permute-start(bf16[2,128,1024]{2,1,0:T(8,128)(2,1)} %pad_maximum_fusion.2), channel_id=1, source_target_pairs={{0,16},{8,24},{16,32},{24,40},{32,48},{40,56},{48,64},{56,72},{64,... | collective-permute-start | bytes 1572872 | tf_op jit(solution)/shard_map/while/body/eval_jaxpr/ppermute | solution.py:13
  1043.1 5.7 collective-permute-start.3
  1074.3 5.6 fusion.116
  1098.2 25.8 %collective-permute-start.1 = (bf16[2,128,1024]{2,1,0:T(8,128)(2,1)}, bf16[2,128,1024]{2,1,0:T(8,128)(2,1)}, u32[]{:S(2)}, u32[]{:S(2)}) collective-permute-start(bf16[2,128,1024]{2,1,0:T(8,128)(2,1)} %pad_maximum_fusion.2), channel_id=1, source_target_pairs={{0,16},{8,24},{16,32},{24,40},{32,48},{40,56},{48,64},{56,72},{64,... | collective-permute-start | bytes 1572872 | tf_op jit(solution)/shard_map/while/body/eval_jaxpr/ppermute | solution.py:13
  1126.1 5.7 collective-permute-start.3
  1157.2 5.6 fusion.116
  1181.1 25.8 %collective-permute-start.1 = (bf16[2,128,1024]{2,1,0:T(8,128)(2,1)}, bf16[2,128,1024]{2,1,0:T(8,128)(2,1)}, u32[]{:S(2)}, u32[]{:S(2)}) collective-permute-start(bf16[2,128,1024]{2,1,0:T(8,128)(2,1)} %pad_maximum_fusion.2), channel_id=1, source_target_pairs={{0,16},{8,24},{16,32},{24,40},{32,48},{40,56},{48,64},{56,72},{64,... | collective-permute-start | bytes 1572872 | tf_op jit(solution)/shard_map/while/body/eval_jaxpr/ppermute | solution.py:13
  1209.1 5.7 collective-permute-start.3
  1240.2 5.6 fusion.116
  1259.1 82.5 %all-reduce.2.cloned.1.call-done = bf16[8,128,128]{2,1,0:T(8,128)(2,1)} async-done(((bf16[8,128,128]{2,1,0:T(8,128)(2,1)}), bf16[8,128,128]{2,1,0:T(8,128)(2,1)}) %all-reduce.2.cloned.1.call-update) | async-done | bytes 262160 | tf_op jit(solution)/shard_map/psum | solution.py:18
  1343.6 40.9 %psum.15 = f32[]{:T(128)} all-reduce(f32[]{:T(128)} %get-tuple-element.363), channel_id=1, replica_groups=mesh['seq'=16,'segment'=8] {'seq'}, use_global_device_ids=true, to_apply=%region_8.9 | all-reduce | flops 1 | bytes 8 | tf_op jit(solution)/shard_map/psum | solution.py:132
  (1039 shorter events, 708.7 us)
Async XLA Ops:
  7.2 1334.3 %all-reduce.2.cloned.1.call-start = ((), (), s32[]{:S(2)}) async-start(), calls=%async_computation | async-start | bytes 524288 | tf_op jit(solution)/shard_map/psum | solution.py:18
  21.6 22.1 %collective-permute-start = (bf16[2,128,1024]{2,1,0:T(8,128)(2,1)}, bf16[2,128,1024]{2,1,0:T(8,128)(2,1)}, u32[]{:S(2)}, u32[]{:S(2)}) collective-permute-start(bf16[2,128,1024]{2,1,0:T(8,128)(2,1)} %pad_maximum_fusion.2), channel_id=1, source_target_pairs={{0,8},{8,16},{16,24},{24,32},{32,40},{40,48},{48,56},{56,64},{64,7... | collective-permute-start | bytes 1572872 | tf_op jit(solution)/shard_map/while/body/eval_jaxpr/ppermute | solution.py:13
  25.8 22.0 %collective-permute-start.1 = (bf16[2,128,1024]{2,1,0:T(8,128)(2,1)}, bf16[2,128,1024]{2,1,0:T(8,128)(2,1)}, u32[]{:S(2)}, u32[]{:S(2)}) collective-permute-start(bf16[2,128,1024]{2,1,0:T(8,128)(2,1)} %pad_maximum_fusion.2), channel_id=1, source_target_pairs={{0,16},{8,24},{16,32},{24,40},{32,48},{40,56},{48,64},{56,72},{64,... | collective-permute-start | bytes 1572872 | tf_op jit(solution)/shard_map/while/body/eval_jaxpr/ppermute | solution.py:13
  30.6 19.1 %collective-permute-start.2 = (bf16[2,128,1024]{2,1,0:T(8,128)(2,1)}, bf16[2,128,1024]{2,1,0:T(8,128)(2,1)}, u32[]{:S(2)}, u32[]{:S(2)}) collective-permute-start(bf16[2,128,1024]{2,1,0:T(8,128)(2,1)} %pad_maximum_fusion.2), channel_id=1, source_target_pairs={{0,32},{8,40},{16,48},{24,56},{32,64},{40,72},{48,80},{56,88},{64,... | collective-permute-start | bytes 1572872 | tf_op jit(solution)/shard_map/while/body/eval_jaxpr/ppermute | solution.py:13
  34.1 21.4 %collective-permute-start.3 = (bf16[2,128,1024]{2,1,0:T(8,128)(2,1)}, bf16[2,128,1024]{2,1,0:T(8,128)(2,1)}, u32[]{:S(2)}, u32[]{:S(2)}) collective-permute-start(bf16[2,128,1024]{2,1,0:T(8,128)(2,1)} %pad_maximum_fusion.2), channel_id=1, source_target_pairs={{0,64},{8,72},{16,80},{24,88},{32,96},{40,104},{48,112},{56,120},{... | collective-permute-start | bytes 1572872 | tf_op jit(solution)/shard_map/while/body/eval_jaxpr/ppermute | solution.py:13
  91.2 43.2 %collective-permute-start = (bf16[2,128,1024]{2,1,0:T(8,128)(2,1)}, bf16[2,128,1024]{2,1,0:T(8,128)(2,1)}, u32[]{:S(2)}, u32[]{:S(2)}) collective-permute-start(bf16[2,128,1024]{2,1,0:T(8,128)(2,1)} %pad_maximum_fusion.2), channel_id=1, source_target_pairs={{0,8},{8,16},{16,24},{24,32},{32,40},{40,48},{48,56},{56,64},{64,7... | collective-permute-start | bytes 1572872 | tf_op jit(solution)/shard_map/while/body/eval_jaxpr/ppermute | solution.py:13
  94.4 41.9 %collective-permute-start.1 = (bf16[2,128,1024]{2,1,0:T(8,128)(2,1)}, bf16[2,128,1024]{2,1,0:T(8,128)(2,1)}, u32[]{:S(2)}, u32[]{:S(2)}) collective-permute-start(bf16[2,128,1024]{2,1,0:T(8,128)(2,1)} %pad_maximum_fusion.2), channel_id=1, source_target_pairs={{0,16},{8,24},{16,32},{24,40},{32,48},{40,56},{48,64},{56,72},{64,... | collective-permute-start | bytes 1572872 | tf_op jit(solution)/shard_map/while/body/eval_jaxpr/ppermute | solution.py:13
  121.6 16.7 %collective-permute-start.2 = (bf16[2,128,1024]{2,1,0:T(8,128)(2,1)}, bf16[2,128,1024]{2,1,0:T(8,128)(2,1)}, u32[]{:S(2)}, u32[]{:S(2)}) collective-permute-start(bf16[2,128,1024]{2,1,0:T(8,128)(2,1)} %pad_maximum_fusion.2), channel_id=1, source_target_pairs={{0,32},{8,40},{16,48},{24,56},{32,64},{40,72},{48,80},{56,88},{64,... | collective-permute-start | bytes 1572872 | tf_op jit(solution)/shard_map/while/body/eval_jaxpr/ppermute | solution.py:13
  123.7 21.1 %collective-permute-start.3 = (bf16[2,128,1024]{2,1,0:T(8,128)(2,1)}, bf16[2,128,1024]{2,1,0:T(8,128)(2,1)}, u32[]{:S(2)}, u32[]{:S(2)}) collective-permute-start(bf16[2,128,1024]{2,1,0:T(8,128)(2,1)} %pad_maximum_fusion.2), channel_id=1, source_target_pairs={{0,64},{8,72},{16,80},{24,88},{32,96},{40,104},{48,112},{56,120},{... | collective-permute-start | bytes 1572872 | tf_op jit(solution)/shard_map/while/body/eval_jaxpr/ppermute | solution.py:13
  180.6 43.5 %collective-permute-start = (bf16[2,128,1024]{2,1,0:T(8,128)(2,1)}, bf16[2,128,1024]{2,1,0:T(8,128)(2,1)}, u32[]{:S(2)}, u32[]{:S(2)}) collective-permute-start(bf16[2,128,1024]{2,1,0:T(8,128)(2,1)} %pad_maximum_fusion.2), channel_id=1, source_target_pairs={{0,8},{8,16},{16,24},{24,32},{32,40},{40,48},{48,56},{56,64},{64,7... | collective-permute-start | bytes 1572872 | tf_op jit(solution)/shard_map/while/body/eval_jaxpr/ppermute | solution.py:13
  183.0 43.0 %collective-permute-start.1 = (bf16[2,128,1024]{2,1,0:T(8,128)(2,1)}, bf16[2,128,1024]{2,1,0:T(8,128)(2,1)}, u32[]{:S(2)}, u32[]{:S(2)}) collective-permute-start(bf16[2,128,1024]{2,1,0:T(8,128)(2,1)} %pad_maximum_fusion.2), channel_id=1, source_target_pairs={{0,16},{8,24},{16,32},{24,40},{32,48},{40,56},{48,64},{56,72},{64,... | collective-permute-start | bytes 1572872 | tf_op jit(solution)/shard_map/while/body/eval_jaxpr/ppermute | solution.py:13
  211.3 16.7 %collective-permute-start.2 = (bf16[2,128,1024]{2,1,0:T(8,128)(2,1)}, bf16[2,128,1024]{2,1,0:T(8,128)(2,1)}, u32[]{:S(2)}, u32[]{:S(2)}) collective-permute-start(bf16[2,128,1024]{2,1,0:T(8,128)(2,1)} %pad_maximum_fusion.2), channel_id=1, source_target_pairs={{0,32},{8,40},{16,48},{24,56},{32,64},{40,72},{48,80},{56,88},{64,... | collective-permute-start | bytes 1572872 | tf_op jit(solution)/shard_map/while/body/eval_jaxpr/ppermute | solution.py:13
  213.4 18.0 %collective-permute-start.3 = (bf16[2,128,1024]{2,1,0:T(8,128)(2,1)}, bf16[2,128,1024]{2,1,0:T(8,128)(2,1)}, u32[]{:S(2)}, u32[]{:S(2)}) collective-permute-start(bf16[2,128,1024]{2,1,0:T(8,128)(2,1)} %pad_maximum_fusion.2), channel_id=1, source_target_pairs={{0,64},{8,72},{16,80},{24,88},{32,96},{40,104},{48,112},{56,120},{... | collective-permute-start | bytes 1572872 | tf_op jit(solution)/shard_map/while/body/eval_jaxpr/ppermute | solution.py:13
  267.1 42.6 %collective-permute-start = (bf16[2,128,1024]{2,1,0:T(8,128)(2,1)}, bf16[2,128,1024]{2,1,0:T(8,128)(2,1)}, u32[]{:S(2)}, u32[]{:S(2)}) collective-permute-start(bf16[2,128,1024]{2,1,0:T(8,128)(2,1)} %pad_maximum_fusion.2), channel_id=1, source_target_pairs={{0,8},{8,16},{16,24},{24,32},{32,40},{40,48},{48,56},{56,64},{64,7... | collective-permute-start | bytes 1572872 | tf_op jit(solution)/shard_map/while/body/eval_jaxpr/ppermute | solution.py:13
  269.5 42.2 %collective-permute-start.1 = (bf16[2,128,1024]{2,1,0:T(8,128)(2,1)}, bf16[2,128,1024]{2,1,0:T(8,128)(2,1)}, u32[]{:S(2)}, u32[]{:S(2)}) collective-permute-start(bf16[2,128,1024]{2,1,0:T(8,128)(2,1)} %pad_maximum_fusion.2), channel_id=1, source_target_pairs={{0,16},{8,24},{16,32},{24,40},{32,48},{40,56},{48,64},{56,72},{64,... | collective-permute-start | bytes 1572872 | tf_op jit(solution)/shard_map/while/body/eval_jaxpr/ppermute | solution.py:13
  297.0 16.7 %collective-permute-start.2 = (bf16[2,128,1024]{2,1,0:T(8,128)(2,1)}, bf16[2,128,1024]{2,1,0:T(8,128)(2,1)}, u32[]{:S(2)}, u32[]{:S(2)}) collective-permute-start(bf16[2,128,1024]{2,1,0:T(8,128)(2,1)} %pad_maximum_fusion.2), channel_id=1, source_target_pairs={{0,32},{8,40},{16,48},{24,56},{32,64},{40,72},{48,80},{56,88},{64,... | collective-permute-start | bytes 1572872 | tf_op jit(solution)/shard_map/while/body/eval_jaxpr/ppermute | solution.py:13
  351.4 38.6 %collective-permute-start = (bf16[2,128,1024]{2,1,0:T(8,128)(2,1)}, bf16[2,128,1024]{2,1,0:T(8,128)(2,1)}, u32[]{:S(2)}, u32[]{:S(2)}) collective-permute-start(bf16[2,128,1024]{2,1,0:T(8,128)(2,1)} %pad_maximum_fusion.2), channel_id=1, source_target_pairs={{0,8},{8,16},{16,24},{24,32},{32,40},{40,48},{48,56},{56,64},{64,7... | collective-permute-start | bytes 1572872 | tf_op jit(solution)/shard_map/while/body/eval_jaxpr/ppermute | solution.py:13
  353.5 38.4 %collective-permute-start.1 = (bf16[2,128,1024]{2,1,0:T(8,128)(2,1)}, bf16[2,128,1024]{2,1,0:T(8,128)(2,1)}, u32[]{:S(2)}, u32[]{:S(2)}) collective-permute-start(bf16[2,128,1024]{2,1,0:T(8,128)(2,1)} %pad_maximum_fusion.2), channel_id=1, source_target_pairs={{0,16},{8,24},{16,32},{24,40},{32,48},{40,56},{48,64},{56,72},{64,... | collective-permute-start | bytes 1572872 | tf_op jit(solution)/shard_map/while/body/eval_jaxpr/ppermute | solution.py:13
  377.2 16.7 %collective-permute-start.2 = (bf16[2,128,1024]{2,1,0:T(8,128)(2,1)}, bf16[2,128,1024]{2,1,0:T(8,128)(2,1)}, u32[]{:S(2)}, u32[]{:S(2)}) collective-permute-start(bf16[2,128,1024]{2,1,0:T(8,128)(2,1)} %pad_maximum_fusion.2), channel_id=1, source_target_pairs={{0,32},{8,40},{16,48},{24,56},{32,64},{40,72},{48,80},{56,88},{64,... | collective-permute-start | bytes 1572872 | tf_op jit(solution)/shard_map/while/body/eval_jaxpr/ppermute | solution.py:13
  379.3 17.1 %collective-permute-start.3 = (bf16[2,128,1024]{2,1,0:T(8,128)(2,1)}, bf16[2,128,1024]{2,1,0:T(8,128)(2,1)}, u32[]{:S(2)}, u32[]{:S(2)}) collective-permute-start(bf16[2,128,1024]{2,1,0:T(8,128)(2,1)} %pad_maximum_fusion.2), channel_id=1, source_target_pairs={{0,64},{8,72},{16,80},{24,88},{32,96},{40,104},{48,112},{56,120},{... | collective-permute-start | bytes 1572872 | tf_op jit(solution)/shard_map/while/body/eval_jaxpr/ppermute | solution.py:13
  432.2 40.8 %collective-permute-start = (bf16[2,128,1024]{2,1,0:T(8,128)(2,1)}, bf16[2,128,1024]{2,1,0:T(8,128)(2,1)}, u32[]{:S(2)}, u32[]{:S(2)}) collective-permute-start(bf16[2,128,1024]{2,1,0:T(8,128)(2,1)} %pad_maximum_fusion.2), channel_id=1, source_target_pairs={{0,8},{8,16},{16,24},{24,32},{32,40},{40,48},{48,56},{56,64},{64,7... | collective-permute-start | bytes 1572872 | tf_op jit(solution)/shard_map/while/body/eval_jaxpr/ppermute | solution.py:13
  434.5 40.4 %collective-permute-start.1 = (bf16[2,128,1024]{2,1,0:T(8,128)(2,1)}, bf16[2,128,1024]{2,1,0:T(8,128)(2,1)}, u32[]{:S(2)}, u32[]{:S(2)}) collective-permute-start(bf16[2,128,1024]{2,1,0:T(8,128)(2,1)} %pad_maximum_fusion.2), channel_id=1, source_target_pairs={{0,16},{8,24},{16,32},{24,40},{32,48},{40,56},{48,64},{56,72},{64,... | collective-permute-start | bytes 1572872 | tf_op jit(solution)/shard_map/while/body/eval_jaxpr/ppermute | solution.py:13
  460.2 16.7 %collective-permute-start.2 = (bf16[2,128,1024]{2,1,0:T(8,128)(2,1)}, bf16[2,128,1024]{2,1,0:T(8,128)(2,1)}, u32[]{:S(2)}, u32[]{:S(2)}) collective-permute-start(bf16[2,128,1024]{2,1,0:T(8,128)(2,1)} %pad_maximum_fusion.2), channel_id=1, source_target_pairs={{0,32},{8,40},{16,48},{24,56},{32,64},{40,72},{48,80},{56,88},{64,... | collective-permute-start | bytes 1572872 | tf_op jit(solution)/shard_map/while/body/eval_jaxpr/ppermute | solution.py:13
  462.3 16.8 %collective-permute-start.3 = (bf16[2,128,1024]{2,1,0:T(8,128)(2,1)}, bf16[2,128,1024]{2,1,0:T(8,128)(2,1)}, u32[]{:S(2)}, u32[]{:S(2)}) collective-permute-start(bf16[2,128,1024]{2,1,0:T(8,128)(2,1)} %pad_maximum_fusion.2), channel_id=1, source_target_pairs={{0,64},{8,72},{16,80},{24,88},{32,96},{40,104},{48,112},{56,120},{... | collective-permute-start | bytes 1572872 | tf_op jit(solution)/shard_map/while/body/eval_jaxpr/ppermute | solution.py:13
  514.9 41.1 %collective-permute-start = (bf16[2,128,1024]{2,1,0:T(8,128)(2,1)}, bf16[2,128,1024]{2,1,0:T(8,128)(2,1)}, u32[]{:S(2)}, u32[]{:S(2)}) collective-permute-start(bf16[2,128,1024]{2,1,0:T(8,128)(2,1)} %pad_maximum_fusion.2), channel_id=1, source_target_pairs={{0,8},{8,16},{16,24},{24,32},{32,40},{40,48},{48,56},{56,64},{64,7... | collective-permute-start | bytes 1572872 | tf_op jit(solution)/shard_map/while/body/eval_jaxpr/ppermute | solution.py:13
  517.3 40.6 %collective-permute-start.1 = (bf16[2,128,1024]{2,1,0:T(8,128)(2,1)}, bf16[2,128,1024]{2,1,0:T(8,128)(2,1)}, u32[]{:S(2)}, u32[]{:S(2)}) collective-permute-start(bf16[2,128,1024]{2,1,0:T(8,128)(2,1)} %pad_maximum_fusion.2), channel_id=1, source_target_pairs={{0,16},{8,24},{16,32},{24,40},{32,48},{40,56},{48,64},{56,72},{64,... | collective-permute-start | bytes 1572872 | tf_op jit(solution)/shard_map/while/body/eval_jaxpr/ppermute | solution.py:13
  543.2 16.7 %collective-permute-start.2 = (bf16[2,128,1024]{2,1,0:T(8,128)(2,1)}, bf16[2,128,1024]{2,1,0:T(8,128)(2,1)}, u32[]{:S(2)}, u32[]{:S(2)}) collective-permute-start(bf16[2,128,1024]{2,1,0:T(8,128)(2,1)} %pad_maximum_fusion.2), channel_id=1, source_target_pairs={{0,32},{8,40},{16,48},{24,56},{32,64},{40,72},{48,80},{56,88},{64,... | collective-permute-start | bytes 1572872 | tf_op jit(solution)/shard_map/while/body/eval_jaxpr/ppermute | solution.py:13
  597.7 41.3 %collective-permute-start = (bf16[2,128,1024]{2,1,0:T(8,128)(2,1)}, bf16[2,128,1024]{2,1,0:T(8,128)(2,1)}, u32[]{:S(2)}, u32[]{:S(2)}) collective-permute-start(bf16[2,128,1024]{2,1,0:T(8,128)(2,1)} %pad_maximum_fusion.2), channel_id=1, source_target_pairs={{0,8},{8,16},{16,24},{24,32},{32,40},{40,48},{48,56},{56,64},{64,7... | collective-permute-start | bytes 1572872 | tf_op jit(solution)/shard_map/while/body/eval_jaxpr/ppermute | solution.py:13
  600.3 40.6 %collective-permute-start.1 = (bf16[2,128,1024]{2,1,0:T(8,128)(2,1)}, bf16[2,128,1024]{2,1,0:T(8,128)(2,1)}, u32[]{:S(2)}, u32[]{:S(2)}) collective-permute-start(bf16[2,128,1024]{2,1,0:T(8,128)(2,1)} %pad_maximum_fusion.2), channel_id=1, source_target_pairs={{0,16},{8,24},{16,32},{24,40},{32,48},{40,56},{48,64},{56,72},{64,... | collective-permute-start | bytes 1572872 | tf_op jit(solution)/shard_map/while/body/eval_jaxpr/ppermute | solution.py:13
  680.6 41.3 %collective-permute-start = (bf16[2,128,1024]{2,1,0:T(8,128)(2,1)}, bf16[2,128,1024]{2,1,0:T(8,128)(2,1)}, u32[]{:S(2)}, u32[]{:S(2)}) collective-permute-start(bf16[2,128,1024]{2,1,0:T(8,128)(2,1)} %pad_maximum_fusion.2), channel_id=1, source_target_pairs={{0,8},{8,16},{16,24},{24,32},{32,40},{40,48},{48,56},{56,64},{64,7... | collective-permute-start | bytes 1572872 | tf_op jit(solution)/shard_map/while/body/eval_jaxpr/ppermute | solution.py:13
  683.3 40.6 %collective-permute-start.1 = (bf16[2,128,1024]{2,1,0:T(8,128)(2,1)}, bf16[2,128,1024]{2,1,0:T(8,128)(2,1)}, u32[]{:S(2)}, u32[]{:S(2)}) collective-permute-start(bf16[2,128,1024]{2,1,0:T(8,128)(2,1)} %pad_maximum_fusion.2), channel_id=1, source_target_pairs={{0,16},{8,24},{16,32},{24,40},{32,48},{40,56},{48,64},{56,72},{64,... | collective-permute-start | bytes 1572872 | tf_op jit(solution)/shard_map/while/body/eval_jaxpr/ppermute | solution.py:13
  709.1 16.7 %collective-permute-start.2 = (bf16[2,128,1024]{2,1,0:T(8,128)(2,1)}, bf16[2,128,1024]{2,1,0:T(8,128)(2,1)}, u32[]{:S(2)}, u32[]{:S(2)}) collective-permute-start(bf16[2,128,1024]{2,1,0:T(8,128)(2,1)} %pad_maximum_fusion.2), channel_id=1, source_target_pairs={{0,32},{8,40},{16,48},{24,56},{32,64},{40,72},{48,80},{56,88},{64,... | collective-permute-start | bytes 1572872 | tf_op jit(solution)/shard_map/while/body/eval_jaxpr/ppermute | solution.py:13
  763.6 41.3 %collective-permute-start = (bf16[2,128,1024]{2,1,0:T(8,128)(2,1)}, bf16[2,128,1024]{2,1,0:T(8,128)(2,1)}, u32[]{:S(2)}, u32[]{:S(2)}) collective-permute-start(bf16[2,128,1024]{2,1,0:T(8,128)(2,1)} %pad_maximum_fusion.2), channel_id=1, source_target_pairs={{0,8},{8,16},{16,24},{24,32},{32,40},{40,48},{48,56},{56,64},{64,7... | collective-permute-start | bytes 1572872 | tf_op jit(solution)/shard_map/while/body/eval_jaxpr/ppermute | solution.py:13
  766.3 40.6 %collective-permute-start.1 = (bf16[2,128,1024]{2,1,0:T(8,128)(2,1)}, bf16[2,128,1024]{2,1,0:T(8,128)(2,1)}, u32[]{:S(2)}, u32[]{:S(2)}) collective-permute-start(bf16[2,128,1024]{2,1,0:T(8,128)(2,1)} %pad_maximum_fusion.2), channel_id=1, source_target_pairs={{0,16},{8,24},{16,32},{24,40},{32,48},{40,56},{48,64},{56,72},{64,... | collective-permute-start | bytes 1572872 | tf_op jit(solution)/shard_map/while/body/eval_jaxpr/ppermute | solution.py:13
  792.1 16.7 %collective-permute-start.2 = (bf16[2,128,1024]{2,1,0:T(8,128)(2,1)}, bf16[2,128,1024]{2,1,0:T(8,128)(2,1)}, u32[]{:S(2)}, u32[]{:S(2)}) collective-permute-start(bf16[2,128,1024]{2,1,0:T(8,128)(2,1)} %pad_maximum_fusion.2), channel_id=1, source_target_pairs={{0,32},{8,40},{16,48},{24,56},{32,64},{40,72},{48,80},{56,88},{64,... | collective-permute-start | bytes 1572872 | tf_op jit(solution)/shard_map/while/body/eval_jaxpr/ppermute | solution.py:13
  846.6 41.3 %collective-permute-start = (bf16[2,128,1024]{2,1,0:T(8,128)(2,1)}, bf16[2,128,1024]{2,1,0:T(8,128)(2,1)}, u32[]{:S(2)}, u32[]{:S(2)}) collective-permute-start(bf16[2,128,1024]{2,1,0:T(8,128)(2,1)} %pad_maximum_fusion.2), channel_id=1, source_target_pairs={{0,8},{8,16},{16,24},{24,32},{32,40},{40,48},{48,56},{56,64},{64,7... | collective-permute-start | bytes 1572872 | tf_op jit(solution)/shard_map/while/body/eval_jaxpr/ppermute | solution.py:13
  849.2 40.6 %collective-permute-start.1 = (bf16[2,128,1024]{2,1,0:T(8,128)(2,1)}, bf16[2,128,1024]{2,1,0:T(8,128)(2,1)}, u32[]{:S(2)}, u32[]{:S(2)}) collective-permute-start(bf16[2,128,1024]{2,1,0:T(8,128)(2,1)} %pad_maximum_fusion.2), channel_id=1, source_target_pairs={{0,16},{8,24},{16,32},{24,40},{32,48},{40,56},{48,64},{56,72},{64,... | collective-permute-start | bytes 1572872 | tf_op jit(solution)/shard_map/while/body/eval_jaxpr/ppermute | solution.py:13
  875.1 16.7 %collective-permute-start.2 = (bf16[2,128,1024]{2,1,0:T(8,128)(2,1)}, bf16[2,128,1024]{2,1,0:T(8,128)(2,1)}, u32[]{:S(2)}, u32[]{:S(2)}) collective-permute-start(bf16[2,128,1024]{2,1,0:T(8,128)(2,1)} %pad_maximum_fusion.2), channel_id=1, source_target_pairs={{0,32},{8,40},{16,48},{24,56},{32,64},{40,72},{48,80},{56,88},{64,... | collective-permute-start | bytes 1572872 | tf_op jit(solution)/shard_map/while/body/eval_jaxpr/ppermute | solution.py:13
  929.5 41.3 %collective-permute-start = (bf16[2,128,1024]{2,1,0:T(8,128)(2,1)}, bf16[2,128,1024]{2,1,0:T(8,128)(2,1)}, u32[]{:S(2)}, u32[]{:S(2)}) collective-permute-start(bf16[2,128,1024]{2,1,0:T(8,128)(2,1)} %pad_maximum_fusion.2), channel_id=1, source_target_pairs={{0,8},{8,16},{16,24},{24,32},{32,40},{40,48},{48,56},{56,64},{64,7... | collective-permute-start | bytes 1572872 | tf_op jit(solution)/shard_map/while/body/eval_jaxpr/ppermute | solution.py:13
  932.2 40.6 %collective-permute-start.1 = (bf16[2,128,1024]{2,1,0:T(8,128)(2,1)}, bf16[2,128,1024]{2,1,0:T(8,128)(2,1)}, u32[]{:S(2)}, u32[]{:S(2)}) collective-permute-start(bf16[2,128,1024]{2,1,0:T(8,128)(2,1)} %pad_maximum_fusion.2), channel_id=1, source_target_pairs={{0,16},{8,24},{16,32},{24,40},{32,48},{40,56},{48,64},{56,72},{64,... | collective-permute-start | bytes 1572872 | tf_op jit(solution)/shard_map/while/body/eval_jaxpr/ppermute | solution.py:13
  958.1 16.7 %collective-permute-start.2 = (bf16[2,128,1024]{2,1,0:T(8,128)(2,1)}, bf16[2,128,1024]{2,1,0:T(8,128)(2,1)}, u32[]{:S(2)}, u32[]{:S(2)}) collective-permute-start(bf16[2,128,1024]{2,1,0:T(8,128)(2,1)} %pad_maximum_fusion.2), channel_id=1, source_target_pairs={{0,32},{8,40},{16,48},{24,56},{32,64},{40,72},{48,80},{56,88},{64,... | collective-permute-start | bytes 1572872 | tf_op jit(solution)/shard_map/while/body/eval_jaxpr/ppermute | solution.py:13
  1012.5 41.3 %collective-permute-start = (bf16[2,128,1024]{2,1,0:T(8,128)(2,1)}, bf16[2,128,1024]{2,1,0:T(8,128)(2,1)}, u32[]{:S(2)}, u32[]{:S(2)}) collective-permute-start(bf16[2,128,1024]{2,1,0:T(8,128)(2,1)} %pad_maximum_fusion.2), channel_id=1, source_target_pairs={{0,8},{8,16},{16,24},{24,32},{32,40},{40,48},{48,56},{56,64},{64,7... | collective-permute-start | bytes 1572872 | tf_op jit(solution)/shard_map/while/body/eval_jaxpr/ppermute | solution.py:13
  1015.2 40.6 %collective-permute-start.1 = (bf16[2,128,1024]{2,1,0:T(8,128)(2,1)}, bf16[2,128,1024]{2,1,0:T(8,128)(2,1)}, u32[]{:S(2)}, u32[]{:S(2)}) collective-permute-start(bf16[2,128,1024]{2,1,0:T(8,128)(2,1)} %pad_maximum_fusion.2), channel_id=1, source_target_pairs={{0,16},{8,24},{16,32},{24,40},{32,48},{40,56},{48,64},{56,72},{64,... | collective-permute-start | bytes 1572872 | tf_op jit(solution)/shard_map/while/body/eval_jaxpr/ppermute | solution.py:13
  1095.5 41.3 %collective-permute-start = (bf16[2,128,1024]{2,1,0:T(8,128)(2,1)}, bf16[2,128,1024]{2,1,0:T(8,128)(2,1)}, u32[]{:S(2)}, u32[]{:S(2)}) collective-permute-start(bf16[2,128,1024]{2,1,0:T(8,128)(2,1)} %pad_maximum_fusion.2), channel_id=1, source_target_pairs={{0,8},{8,16},{16,24},{24,32},{32,40},{40,48},{48,56},{56,64},{64,7... | collective-permute-start | bytes 1572872 | tf_op jit(solution)/shard_map/while/body/eval_jaxpr/ppermute | solution.py:13
  1098.2 40.6 %collective-permute-start.1 = (bf16[2,128,1024]{2,1,0:T(8,128)(2,1)}, bf16[2,128,1024]{2,1,0:T(8,128)(2,1)}, u32[]{:S(2)}, u32[]{:S(2)}) collective-permute-start(bf16[2,128,1024]{2,1,0:T(8,128)(2,1)} %pad_maximum_fusion.2), channel_id=1, source_target_pairs={{0,16},{8,24},{16,32},{24,40},{32,48},{40,56},{48,64},{56,72},{64,... | collective-permute-start | bytes 1572872 | tf_op jit(solution)/shard_map/while/body/eval_jaxpr/ppermute | solution.py:13
  1124.0 16.7 %collective-permute-start.2 = (bf16[2,128,1024]{2,1,0:T(8,128)(2,1)}, bf16[2,128,1024]{2,1,0:T(8,128)(2,1)}, u32[]{:S(2)}, u32[]{:S(2)}) collective-permute-start(bf16[2,128,1024]{2,1,0:T(8,128)(2,1)} %pad_maximum_fusion.2), channel_id=1, source_target_pairs={{0,32},{8,40},{16,48},{24,56},{32,64},{40,72},{48,80},{56,88},{64,... | collective-permute-start | bytes 1572872 | tf_op jit(solution)/shard_map/while/body/eval_jaxpr/ppermute | solution.py:13
  1178.5 41.3 %collective-permute-start = (bf16[2,128,1024]{2,1,0:T(8,128)(2,1)}, bf16[2,128,1024]{2,1,0:T(8,128)(2,1)}, u32[]{:S(2)}, u32[]{:S(2)}) collective-permute-start(bf16[2,128,1024]{2,1,0:T(8,128)(2,1)} %pad_maximum_fusion.2), channel_id=1, source_target_pairs={{0,8},{8,16},{16,24},{24,32},{32,40},{40,48},{48,56},{56,64},{64,7... | collective-permute-start | bytes 1572872 | tf_op jit(solution)/shard_map/while/body/eval_jaxpr/ppermute | solution.py:13
  1181.1 40.6 %collective-permute-start.1 = (bf16[2,128,1024]{2,1,0:T(8,128)(2,1)}, bf16[2,128,1024]{2,1,0:T(8,128)(2,1)}, u32[]{:S(2)}, u32[]{:S(2)}) collective-permute-start(bf16[2,128,1024]{2,1,0:T(8,128)(2,1)} %pad_maximum_fusion.2), channel_id=1, source_target_pairs={{0,16},{8,24},{16,32},{24,40},{32,48},{40,56},{48,64},{56,72},{64,... | collective-permute-start | bytes 1572872 | tf_op jit(solution)/shard_map/while/body/eval_jaxpr/ppermute | solution.py:13
  (182 other events, 907.9 us)
Sparse Core Ops, SparseCore 0:
  1259.2 82.3 all-reduce.1
where the time goes:
time: 1410 us; the launch traced here: 1390 us
  starting transfers between devices  557 us (40%)
  local copies, waits for them, and re-layouts  348 us (25%)
  matrix products  232 us (16%)
  waiting for transfers between devices  156 us (11%)
  blocking collectives  40.9 us (3%)
  other arithmetic  36.3 us (3%)
  between operations  18.4 us (1%)
    ppermute x75, starting transfers between devices, from_behind(): lax.ppermute(value, axis, [(source, source + steps) for source in range(l...  557 us
    slice x120, local copies, waits for them, and re-layouts, section(): key_parts.append(arrived[0])  204 us
    sub x15, matrix products, attend(): expon = jnp.exp(scores - peak)  83.5 us
    psum x1, waiting for transfers between devices, from_root(): return lax.psum(jnp.where(mine, value, jnp.zeros_like(value)), axis)  82.5 us
    while x465, local copies, waits for them, and re-layouts  78.4 us
    ppermute x75, waiting for transfers between devices, from_behind(): lax.ppermute(value, axis, [(source, source + steps) for source in range(l...  73.8 us
    dot_general x15, matrix products, attend(): jnp.einsum('hqk,khe->qhe', weights, vhead, preferred_element_type=jnp.flo...  63.5 us
    psum x1, blocking collectives, per_device(): total = lax.psum(partial_sum, 'seq')  40.9 us
  transfers between devices with their start and end apart: 76, of which 22 were waited for; matrix products, arithmetic and copies ran while one was open for 13% of the time, Pallas kernels for 0%

commit v1 on v0

v1 whole, which is shorter than its diff:
```python
import jax
import jax.numpy as jnp
from jax import lax
from jax.experimental import pallas as pl
from jax.experimental.pallas import tpu as pltpu
from jax.sharding import PartitionSpec as P

TICKS = 8
PAIRS = 8
CHUNKS = 4
AHEAD = 2
NEG = -1e30


def rms(values, gain):
    meansq = jnp.mean(values * values, axis=-1, keepdims=True) + 1e-05
    return (values * lax.rsqrt(meansq) * gain).astype(jnp.bfloat16)


def rows_of(ref):
    return jnp.concatenate([ref[c] for c in range(CHUNKS)], axis=1)


def kernel(
    base_ref,
    forcing_ref,
    theta_ref,
    perturb_ref,
    order_ref,
    w_force_ref,
    gain_ref,
    wq_hbm,
    wk_hbm,
    wv_hbm,
    wo_hbm,
    mask_ref,
    out_gain_ref,
    w_read_ref,
    observed_ref,
    pred_out,
    fit_out,
    wq,
    wk,
    wv,
    wo,
    x_own,
    x_cross,
    x_out,
    starts,
    normed,
    q_buf,
    k_own,
    v_own,
    k_cross,
    v_cross,
    ctx,
    causal,
    bias,
    obs,
    pred_send,
    pred_recv,
    acc,
    fit_send,
    fit_recv,
    w_sem,
    own_sem,
    cross_sem,
    send_own_sem,
    send_cross_sem,
    start_sem,
    bias_sem,
    bias_send_sem,
    obs_sem,
    obs_send_sem,
    pred_sem,
    pred_send_sem,
    fit_sem,
    fit_send_sem,
):
    seq = lax.axis_index("seq")
    seg = lax.axis_index("segment")
    lane = seq % 2
    member = seq // 2
    home = seq // 2
    other = seq + 1 - 2 * lane
    last = 7

    def remote(src, dst, send, recv, to_seq, to_seg):
        return pltpu.make_async_remote_copy(
            src_ref=src,
            dst_ref=dst,
            send_sem=send,
            recv_sem=recv,
            device_id={"seq": to_seq, "segment": to_seg},
            device_id_type=pl.DeviceIdType.MESH,
        )

    loads = [
        pltpu.make_async_copy(hbm.at[0], vmem, w_sem.at[i])
        for i, (hbm, vmem) in enumerate(((wq_hbm, wq), (wk_hbm, wk), (wv_hbm, wv), (wo_hbm, wo)))
    ]
    for load in loads:
        load.start()

    def send_start(m, _):
        target = 2 * m + lane

        @pl.when(target != seq)
        def _():
            remote(
                starts.at[m], x_own.at[home], start_sem.at[m], own_sem.at[home], target, 0
            ).start()

        return 0

    def make_start(m, _):
        theta = theta_ref[...] + 0.5 * perturb_ref[pl.ds(order_ref[m], 1), :]
        drive = forcing_ref[...] * theta
        high = drive.astype(jnp.bfloat16)
        rest = drive - high.astype(jnp.float32)
        middle = rest.astype(jnp.bfloat16)
        low = (rest - middle.astype(jnp.float32)).astype(jnp.bfloat16)
        for c in range(CHUNKS):
            columns = slice(256 * c, 256 * (c + 1))
            w = w_force_ref[:, columns]
            lifted = jnp.dot(low, w, preferred_element_type=jnp.float32)
            lifted += jnp.dot(middle, w, preferred_element_type=jnp.float32)
            lifted += jnp.dot(high, w, preferred_element_type=jnp.float32)
            starts[m, c] = (base_ref[:, columns].astype(jnp.float32) + lifted).astype(jnp.bfloat16)

        @pl.when(home < AHEAD)
        def _():
            send_start(m, 0)

        return 0

    @pl.when(seg == 0)
    def _():
        lax.fori_loop(0, 8, make_start, 0)
        x_own[home] = starts[member]

    for level in range(4):
        usable = (mask_ref[0, level] == 1) & (seq >= 2**level)
        row = jnp.full((8, 128), jnp.where(usable, 0.0, NEG), jnp.float32)
        bias[home, :, 128 * level : 128 * (level + 1)] = row

    def send_bias(j, _):
        target = 2 * j + lane

        @pl.when(target != seq)
        def _():
            remote(
                bias.at[home], bias.at[home], bias_send_sem.at[j], bias_sem.at[home], target, seg
            ).start()

        return 0

    lax.fori_loop(0, 8, send_bias, 0)

    def send_obs(j, _):
        target = 2 * j + lane

        @pl.when(target != seq)
        def _():
            remote(
                obs.at[home], obs.at[home], obs_send_sem.at[j], obs_sem.at[home], target, last
            ).start()

        return 0

    @pl.when(seg == last)
    def _():
        obs[home] = observed_ref[...]
        lax.fori_loop(0, 8, send_obs, 0)

    row = lax.broadcasted_iota(jnp.int32, (256, 128), 0) % 128
    column = lax.broadcasted_iota(jnp.int32, (256, 128), 1)
    causal[...] = jnp.where(column <= row, 0.0, NEG)
    acc[...] = jnp.zeros_like(acc)

    @pl.when(lane == 0)
    def _():
        x_cross[0] = jnp.zeros_like(x_cross[0])

    for load in loads:
        load.wait()

    left = lax.broadcasted_iota(jnp.int32, (128, 128), 1) < 64
    ones = jnp.ones((640, 128), jnp.bfloat16)

    def tick(t, _):
        @pl.when((seg == 0) & (home >= AHEAD) & (t == home - AHEAD))
        def _():
            lax.fori_loop(0, 8, send_start, 0)

        @pl.when((seg > 0) | (t != home))
        def _():
            pltpu.make_async_copy(x_own.at[t], x_own.at[t], own_sem.at[t]).wait()

        @pl.when((seg == 0) & (t + lane < TICKS))
        def _():
            remote(
                x_own.at[t],
                x_cross.at[t + lane],
                send_cross_sem.at[t],
                cross_sem.at[t + lane],
                other,
                0,
            ).start()

        x = rows_of(x_own.at[t]).astype(jnp.float32)
        gain = gain_ref[...]
        normed[0:128] = rms(x, gain)

        @pl.when((lane == 1) | (t > 0))
        def _():
            pltpu.make_async_copy(x_cross.at[t], x_cross.at[t], cross_sem.at[t]).wait()

        normed[128:256] = rms(rows_of(x_cross.at[t]).astype(jnp.float32), gain)

        for c in range(CHUNKS):
            columns = slice(256 * c, 256 * (c + 1))
            q = jnp.dot(normed[0:128], wq[:, columns], preferred_element_type=jnp.float32) * 0.125
            k = jnp.dot(normed[...], wk[:, columns], preferred_element_type=jnp.float32)
            v = jnp.dot(normed[...], wv[:, columns], preferred_element_type=jnp.float32)
            for i in range(2):
                p = 2 * c + i
                part = slice(128 * i, 128 * (i + 1))
                q_buf[p, 0:128] = jnp.where(left, q[:, part], 0.0).astype(jnp.bfloat16)
                q_buf[p, 128:256] = jnp.where(left, 0.0, q[:, part]).astype(jnp.bfloat16)
                k_own[t, p] = k[0:128, part].astype(jnp.bfloat16)
                k_cross[p] = k[128:256, part].astype(jnp.bfloat16)
                v_own[t, p] = v[0:128, part].astype(jnp.bfloat16)
                v_cross[p] = v[128:256, part].astype(jnp.bfloat16)

        @pl.when(t != home)
        def _():
            pltpu.make_async_copy(bias.at[t], bias.at[t], bias_sem.at[t]).wait()

        behind = [jnp.maximum(t - offset, 0) for offset in (1, 2, 4)]

        def attend(p):
            keys = jnp.concatenate(
                [k_own[t, p], k_cross[p]] + [k_own[index, p] for index in behind], axis=0
            )
            values = jnp.concatenate(
                [v_own[t, p], v_cross[p]] + [v_own[index, p] for index in behind], axis=0
            )
            scores = lax.dot_general(
                q_buf[p], keys, (((1,), (1,)), ((), ())), preferred_element_type=jnp.float32
            )
            scores = jnp.concatenate(
                [scores[:, 0:128] + causal[...], scores[:, 128:640] + bias[t, 0:1, :]], axis=1
            )
            peak = jnp.max(scores, axis=-1, keepdims=True)
            expon = jnp.exp(scores - peak).astype(jnp.bfloat16)
            both = jnp.dot(
                expon, jnp.concatenate([values, ones], axis=1), preferred_element_type=jnp.float32
            )
            mixed = both[:, 0:128] / both[:, 128:256]
            ctx[p] = jnp.where(left, mixed[0:128], mixed[128:256]).astype(jnp.bfloat16)

        def attend_two(i, _):
            attend(2 * i)
            attend(2 * i + 1)
            return 0

        lax.fori_loop(0, PAIRS // 2, attend_two, 0)

        context = jnp.concatenate([ctx[p] for p in range(PAIRS)], axis=1)
        for c in range(CHUNKS):
            columns = slice(256 * c, 256 * (c + 1))
            mixed = jnp.dot(context, wo[:, columns], preferred_element_type=jnp.float32)
            x_out[t, c] = (x_own[t, c].astype(jnp.float32) + mixed).astype(jnp.bfloat16)

            @pl.when(seg < last)
            def _():
                remote(
                    x_out.at[t, c], x_own.at[t, c], send_own_sem.at[t], own_sem.at[t], seq, seg + 1
                ).start()

            @pl.when((seg < last) & (t + lane < TICKS))
            def _():
                remote(
                    x_out.at[t, c],
                    x_cross.at[t + lane, c],
                    send_cross_sem.at[t + TICKS],
                    cross_sem.at[t + lane],
                    other,
                    seg + 1,
                ).start()

        @pl.when(seg == last)
        def _():
            final = rms(rows_of(x_out.at[t]).astype(jnp.float32), out_gain_ref[...])
            predicted = jnp.dot(final, w_read_ref[...], preferred_element_type=jnp.float32)
            block = 2 * t + lane
            pred_send[t] = predicted

            @pl.when((block != seq) | (member != last))
            def _():
                remote(
                    pred_send.at[t], pred_recv, pred_send_sem.at[t], pred_sem, block, member
                ).start()

            @pl.when((block == seq) & (member == last))
            def _():
                pred_recv[...] = predicted

            @pl.when(t != home)
            def _():
                pltpu.make_async_copy(obs.at[t], obs.at[t], obs_sem.at[t]).wait()

            errors = predicted - obs[t]
            hours = lax.broadcasted_iota(jnp.int32, (128, 128), 0) + block * 128
            weight = 1.0 + hours.astype(jnp.float32) * (2.0 / 2047.0)
            squares = weight * errors * errors
            acc[...] += jnp.sum(squares.reshape(16, 8, 128), axis=0)

        return 0

    lax.fori_loop(0, TICKS, tick, 0)

    def send_fit(j, _):
        @pl.when((j != seq) | (member != last))
        def _():
            remote(
                fit_send, fit_recv.at[lane], fit_send_sem.at[j], fit_sem.at[lane], j, member
            ).start()

        return 0

    def sent_fit(j, _):
        @pl.when((j != seq) | (member != last))
        def _():
            remote(
                fit_send, fit_recv.at[lane], fit_send_sem.at[j], fit_sem.at[lane], j, member
            ).wait_send()

        return 0

    @pl.when(seg == last)
    def _():
        fit_send[...] = acc[...]
        lax.fori_loop(0, 16, send_fit, 0)

        @pl.when(member == last)
        def _():
            fit_recv[lane] = acc[...]

    def sent_tick(t, _):
        @pl.when(seg < last)
        def _():
            pltpu.make_async_copy(x_out.at[t], x_out.at[t], send_own_sem.at[t]).wait()

            @pl.when(t + lane < TICKS)
            def _():
                pltpu.make_async_copy(x_out.at[t], x_out.at[t], send_cross_sem.at[t + TICKS]).wait()

        @pl.when((seg == 0) & (t + lane < TICKS))
        def _():
            pltpu.make_async_copy(x_own.at[t], x_own.at[t], send_cross_sem.at[t]).wait()

        @pl.when((seg == 0) & (2 * t + lane != seq))
        def _():
            pltpu.make_async_copy(starts.at[t], starts.at[t], start_sem.at[t]).wait()

        @pl.when(2 * t + lane != seq)
        def _():
            pltpu.make_async_copy(bias.at[home], bias.at[home], bias_send_sem.at[t]).wait()

        @pl.when(seg == last)
        def _():
            @pl.when(2 * t + lane != seq)
            def _():
                pltpu.make_async_copy(obs.at[home], obs.at[home], obs_send_sem.at[t]).wait()

            @pl.when((2 * t + lane != seq) | (member != last))
            def _():
                pltpu.make_async_copy(pred_send.at[t], pred_send.at[t], pred_send_sem.at[t]).wait()

        return 0

    lax.fori_loop(0, TICKS, sent_tick, 0)

    @pl.when(seg == last)
    def _():
        lax.fori_loop(0, 16, sent_fit, 0)

    @pl.when((seg != last) | (member != last))
    def _():
        pltpu.make_async_copy(pred_recv, pred_recv, pred_sem).wait()

    for source in range(2):

        @pl.when((seg != last) | (seq != 14 + source))
        def _():
            pltpu.make_async_copy(fit_recv.at[source], fit_recv.at[source], fit_sem.at[source]).wait()

    pred_out[...] = pred_recv[...]
    total = jnp.sum(fit_recv[0] + fit_recv[1])
    fit_out[0] = -total / (2048.0 * 128.0)


def per_device(
    base_state,
    forcing,
    theta_base,
    perturb,
    order,
    w_force,
    attn_gain,
    w_query,
    w_key,
    w_value,
    w_out,
    block_mask,
    out_gain,
    w_read,
    observed,
):
    vmem = pl.BlockSpec(memory_space=pltpu.VMEM)
    smem = pl.BlockSpec(memory_space=pltpu.SMEM)
    hbm = pl.BlockSpec(memory_space=pl.ANY)
    bf16, f32 = jnp.bfloat16, jnp.float32
    dma = pltpu.SemaphoreType.DMA
    predictions, fitness = pl.pallas_call(
        kernel,
        out_shape=(
            jax.ShapeDtypeStruct((128, 128), f32),
            jax.ShapeDtypeStruct((1,), f32),
        ),
        in_specs=[vmem, vmem, vmem, vmem, smem, vmem, vmem, hbm, hbm, hbm, hbm, smem, vmem, vmem, vmem],
        out_specs=(vmem, smem),
        scratch_shapes=[
            pltpu.VMEM((1024, 1024), bf16),
            pltpu.VMEM((1024, 1024), bf16),
            pltpu.VMEM((1024, 1024), bf16),
            pltpu.VMEM((1024, 1024), bf16),
            pltpu.VMEM((TICKS, CHUNKS, 128, 256), bf16),
            pltpu.VMEM((TICKS, CHUNKS, 128, 256), bf16),
            pltpu.VMEM((TICKS, CHUNKS, 128, 256), bf16),
            pltpu.VMEM((8, CHUNKS, 128, 256), bf16),
            pltpu.VMEM((256, 1024), bf16),
            pltpu.VMEM((PAIRS, 256, 128), bf16),
            pltpu.VMEM((TICKS, PAIRS, 128, 128), bf16),
            pltpu.VMEM((TICKS, PAIRS, 128, 128), bf16),
            pltpu.VMEM((PAIRS, 128, 128), bf16),
            pltpu.VMEM((PAIRS, 128, 128), bf16),
            pltpu.VMEM((PAIRS, 128, 128), bf16),
            pltpu.VMEM((256, 128), f32),
            pltpu.VMEM((TICKS, 8, 512), f32),
            pltpu.VMEM((TICKS, 128, 128), f32),
            pltpu.VMEM((TICKS, 128, 128), f32),
            pltpu.VMEM((128, 128), f32),
            pltpu.VMEM((8, 128), f32),
            pltpu.VMEM((8, 128), f32),
            pltpu.VMEM((2, 8, 128), f32),
            dma((4,)),
            dma((TICKS,)),
            dma((TICKS,)),
            dma((TICKS,)),
            dma((2 * TICKS,)),
            dma((8,)),
            dma((TICKS,)),
            dma((8,)),
            dma((TICKS,)),
            dma((8,)),
            dma,
            dma((TICKS,)),
            dma((2,)),
            dma((16,)),
        ],
        compiler_params=pltpu.CompilerParams(
            has_side_effects=True, vmem_limit_bytes=48 * 1024 * 1024
        ),
    )(
        base_state,
        forcing,
        theta_base.reshape(1, -1),
        perturb,
        order,
        w_force,
        attn_gain,
        w_query,
        w_key,
        w_value,
        w_out,
        block_mask,
        out_gain.reshape(1, -1),
        w_read,
        observed,
    )
    return predictions[None], fitness


def solution(mesh):
    placed = (
        P("seq", None),
        P("seq", None),
        P(),
        P(),
        P(),
        P(),
        P("segment", None),
        P("segment", None, None),
        P("segment", None, None),
        P("segment", None, None),
        P("segment", None, None),
        P("seq", None),
        P(),
        P(),
        P("seq", None),
    )
    return jax.shard_map(
        per_device,
        mesh=mesh,
        in_specs=placed,
        out_specs=(P("segment", "seq", None), P("segment")),
        check_vma=False,
    )
```

time: 1410 us -> 193 us (0.14); the launches traced: 1390 us -> 193 us
  starting transfers between devices: 557 us -> 0 us
  local copies, waits for them, and re-layouts: 348 us -> 12.4 us
  matrix products: 232 us -> 0 us
  Pallas kernels: 0 us -> 178 us
  waiting for transfers between devices: 156 us -> 0 us
  blocking collectives: 40.9 us -> 0 us
  other arithmetic: 36.3 us -> 0 us
  between operations: 18.4 us -> 2.43 us
    ppermute x75 -> x0, starting transfers between devices: 557 us -> none  [from_behind(): lax.ppermute(value, axis, [(source, source + steps) for source in range(l...]
    slice x181 -> x0, local copies, waits for them, and re-layouts: 225 us -> none  [the longest x120 204 us: section(): key_parts.append(arrived[0])]
    pallas_call x0 -> x1, Pallas kernels: none -> 178 us  [per_device(): pl.pallas_call(kernel, out_shape=(jax.ShapeDtypeStruct((128, 128), f32),...]
    dot_general x92 -> x0, matrix products: 148 us -> none  [the longest x15 63.5 us: attend(): jnp.einsum('hqk,khe->qhe', weights, vhead, preferred_element_type=jnp.flo...]
    sub x15 -> x0, matrix products: 83.5 us -> none  [attend(): expon = jnp.exp(scores - peak)]
    psum x1 -> x0, waiting for transfers between devices: 82.5 us -> none  [from_root(): return lax.psum(jnp.where(mine, value, jnp.zeros_like(value)), axis)]
    while x465 -> x0, local copies, waits for them, and re-layouts: 78.4 us -> none
    ppermute x75 -> x0, waiting for transfers between devices: 73.8 us -> none  [from_behind(): lax.ppermute(value, axis, [(source, source + steps) for source in range(l...]
  transfers between devices with their start and end apart: 76 -> 0, of which waited for: 22 -> 0; matrix products, arithmetic and copies ran while one was open for 13% -> 0% of each run, Pallas kernels for 0% -> 0%
where the time goes in v1:
time: 193 us
  Pallas kernels  178 us (92%)
  local copies, waits for them, and re-layouts  12.4 us (6%)
  between operations  2.43 us (1%)
    pallas_call x1, Pallas kernels, per_device(): pl.pallas_call(kernel, out_shape=(jax.ShapeDtypeStruct((128, 128), f32),...  178 us
    unnamed x26, local copies, waits for them, and re-layouts  12.4 us

profile of v1, /device:TPU:64, one launch (start us, length us, event | category | flops | bytes accessed | tf_op | source)
XLA Modules:
  0.0 193.0 jit_solution(15737827831521490821)
XLA Ops:
  0.6 0.8 copy.17.forcing_ref
  1.5 0.0 copy-start
  1.5 1.6 copy-done
  3.1 0.0 copy-start.1
  3.1 1.6 copy-done.1
  4.7 0.0 copy-start.2
  4.7 0.9 copy-done.2
  5.6 0.0 copy-start.3
  5.6 0.9 copy-done.3
  6.6 0.0 copy-start.4
  6.6 0.9 copy-done.4
  7.5 0.0 copy-start.5
  7.5 0.8 copy-done.5
  8.3 0.0 copy-start.6
  8.3 0.7 copy-done.6
  9.0 0.0 copy-start.7
  9.0 0.7 copy-done.7
  9.7 0.0 copy-start.8
  9.7 0.7 copy-done.8
  10.4 0.0 copy-start.9
  10.4 0.7 copy-done.9
  11.1 0.0 copy-start.10
  11.1 0.7 copy-done.10
  11.7 0.0 copy-start.11
  11.7 0.7 copy-done.11
  12.4 178.2 %shard_map.158 = (f32[128,128]{1,0:T(8,128)S(1)}, f32[1]{0:T(128)}) custom-call(bf16[128,1024]{1,0:T(8,128)(2,1)S(1)} %copy-done.2, f32[128,64]{1,0:T(8,128)S(1)} %copy.17.forcing_ref, f32[1,64]{1,0:T(1,128)S(1)} %bitcast.5, f32[32,64]{1,0:T(8,128)S(1)} %copy-done.6, s32[32]{0:T(128)S(1)} %copy-done.10, bf16[64,1024]{1,0:T(8,128)(2,1)S(1)} %copy-done.4, ...), custom_call_target="tpu_custom_call" | custom-call | tf_op jit(solution)/shard_map/pallas_call | solution.py:427
  190.6 0.6 copy.20
Async XLA Ops:
  1.5 1.6 copy-start
  3.1 1.6 copy-start.1
  4.7 0.9 copy-start.2
  5.6 0.9 copy-start.3
  6.6 0.9 copy-start.4
  7.5 0.8 copy-start.5
  8.3 0.7 copy-start.6
  9.0 0.7 copy-start.7
  9.7 0.7 copy-start.8
  10.4 0.7 copy-start.9
  11.1 0.7 copy-start.10
  11.7 0.7 copy-start.11

commit v2 on v1

v2 whole, which is shorter than its diff:
```python
import jax
import jax.numpy as jnp
from jax import lax
from jax.experimental import pallas as pl
from jax.experimental.pallas import tpu as pltpu
from jax.sharding import PartitionSpec as P

TICKS = 8
PAIRS = 8
CHUNKS = 4
UNROLL = 4
NEG = -1e30


def rms(values, gain):
    meansq = jnp.mean(values * values, axis=-1, keepdims=True) + 1e-05
    return (values * lax.rsqrt(meansq) * gain).astype(jnp.bfloat16)


def rows_of(ref):
    return jnp.concatenate([ref[c] for c in range(CHUNKS)], axis=1)


def kernel(
    base_hbm,
    forcing_hbm,
    theta_hbm,
    perturb_hbm,
    order_hbm,
    w_force_hbm,
    gain_hbm,
    wq_hbm,
    wk_hbm,
    wv_hbm,
    wo_hbm,
    mask_hbm,
    out_gain_hbm,
    w_read_hbm,
    observed_hbm,
    pred_out,
    fit_out,
    base_ref,
    forcing_ref,
    theta_ref,
    perturb_ref,
    order_ref,
    w_force_ref,
    gain_ref,
    mask_ref,
    out_gain_ref,
    w_read_ref,
    wq,
    wk,
    wv,
    wo,
    x_own,
    x_out,
    start,
    normed,
    q_buf,
    k_own,
    v_own,
    k_cross,
    v_cross,
    ctx,
    causal,
    bias,
    obs,
    pred_send,
    pred_recv,
    acc,
    fit_send,
    fit_recv,
    load_sem,
    w_sem,
    w_send_sem,
    own_sem,
    send_own_sem,
    cross_sem,
    send_cross_sem,
    start_sem,
    bias_sem,
    bias_send_sem,
    obs_sem,
    obs_send_sem,
    pred_sem,
    pred_send_sem,
    fit_sem,
    fit_send_sem,
    token,
):
    seq = lax.axis_index("seq")
    seg = lax.axis_index("segment")
    member = seq // 2
    place = seq % 2
    plane = seg // 2
    lane = seg % 2
    sibling = seg + 1 - 2 * lane
    second = (place + plane) % 2
    stage = 2 * plane + second
    owner = lane == second
    last = 7
    next_seq = seq + (1 - second) * (1 - 2 * place)
    next_seg = seg + 2 * second
    home = seq // 2
    slot = 2 * ((plane + 8 - home) % 4) + lane
    parity = seq % 2
    is_start = seq + seg == 0
    keeps = parity == lane
    final = (stage == last) & (place == 0)

    def peer(to_seq, to_seg):
        return {"seq": to_seq, "segment": to_seg}

    def remote(src, dst, send, recv, to_seq, to_seg):
        return pltpu.make_async_remote_copy(
            src_ref=src,
            dst_ref=dst,
            send_sem=send,
            recv_sem=recv,
            device_id=peer(to_seq, to_seg),
            device_id_type=pl.DeviceIdType.MESH,
        )

    def arrived(ref, sem):
        pltpu.make_async_copy(ref, ref, sem).wait()

    def signal(sem, to_seq, to_seg):
        pl.semaphore_signal(
            sem, inc=1, device_id=peer(to_seq, to_seg), device_id_type=pl.DeviceIdType.MESH
        )

    first = [
        (base_hbm, base_ref),
        (forcing_hbm, forcing_ref),
        (theta_hbm, theta_ref),
        (perturb_hbm, perturb_ref),
        (order_hbm, order_ref),
        (w_force_hbm, w_force_ref),
        (mask_hbm, mask_ref),
        (out_gain_hbm, out_gain_ref),
        (w_read_hbm, w_read_ref),
    ]
    own_obs = pltpu.make_async_copy(observed_hbm, obs.at[home], load_sem.at[len(first)])
    loads = [
        pltpu.make_async_copy(source, target, load_sem.at[i])
        for i, (source, target) in enumerate(first)
    ]
    for load in loads:
        load.start()

    @pl.when(keeps)
    def _():
        own_obs.start()

    weights = [
        (gain_hbm, gain_ref),
        (wk_hbm.at[0], wk),
        (wv_hbm.at[0], wv),
        (wq_hbm.at[0], wq),
        (wo_hbm.at[0], wo),
    ]

    @pl.when(owner)
    def _():
        for i, (source, target) in enumerate(weights):
            pltpu.make_async_copy(source, target, w_sem.at[i]).start()

    barrier = pltpu.get_barrier_semaphore()
    signal(barrier, seq, sibling)

    @pl.when(stage > 0)
    def _():
        signal(barrier, seq + second * (1 - 2 * place), seg - 2 * (1 - second))

    def greet(t, _):
        source = 2 * t + lane

        @pl.when(source != seq)
        def _():
            signal(barrier, source, seg)

            @pl.when(final)
            def _():
                signal(barrier, source, seg)

        @pl.when((stage == 0) & ((seq + seg > 0) | (t > 0)))
        def _():
            signal(barrier, source, 2 * ((member // 2 + t) % 4) + member % 2)

        return 0

    lax.fori_loop(0, TICKS, greet, 0)

    before = home - 3 + plane // 3
    after = home + 3 - (plane % 2) * (1 - plane // 3)
    follows = (plane > 0) & (before >= 0)
    leads = (plane > 0) & (after < 8)
    before_seg = 2 * (plane % 3 + 1) + lane
    after_seg = 2 * ((plane + 1) % 3 + 1) + lane

    @pl.when(follows)
    def _():
        signal(barrier, 2 * before + parity, before_seg)

    for source in range(2):

        @pl.when((seq != 2 * seg) | (seg != 6 + source))
        def _():
            signal(barrier, 2 * seg, 6 + source)

    ends = stage // last
    apart = ((member - seg) * (member - seg) + 63) // 64
    expected = 2 - ends + (seq + seg + 126) // 127
    expected += ((plane + 2) // 3) * (1 - after // 8)
    expected += (1 - (parity + lane) % 2) * (15 + (plane // 3) * (7 + lane))
    expected += ends * (15 + apart)
    pl.semaphore_wait(barrier, expected)

    @pl.when(owner)
    def _():
        for i, (source, target) in enumerate(weights):
            remote(source, target, w_send_sem.at[i], w_sem.at[i], seq, sibling).start()

    for load in loads:
        load.wait()

    def start_copy():
        return remote(start, x_own.at[home], start_sem, own_sem.at[home], 2 * slot, parity)

    theta = theta_ref[...] + 0.5 * perturb_ref[pl.ds(order_ref[slot], 1), :]
    drive = forcing_ref[...].T * theta
    high = drive.astype(jnp.bfloat16)
    rest = drive - high.astype(jnp.float32)
    middle = rest.astype(jnp.bfloat16)
    low = (rest - middle.astype(jnp.float32)).astype(jnp.bfloat16)
    for c in range(CHUNKS):
        columns = slice(256 * c, 256 * (c + 1))
        w = w_force_ref[:, columns]
        lifted = jnp.dot(low, w, preferred_element_type=jnp.float32)
        lifted += jnp.dot(middle, w, preferred_element_type=jnp.float32)
        lifted += jnp.dot(high, w, preferred_element_type=jnp.float32)
        start[c] = (base_ref[:, columns].astype(jnp.float32) + lifted).astype(jnp.bfloat16)

    @pl.when(is_start)
    def _():
        x_own[0] = start[...]

    @pl.when((seq + seg > 0) & jnp.logical_not(follows))
    def _():
        start_copy().start()

    def send_bias(j, _):
        @pl.when(j != seq)
        def _():
            remote(
                bias.at[home], bias.at[home], bias_send_sem.at[j], bias_sem.at[home], j, seg
            ).start()

        return 0

    def send_obs(j, _):
        @pl.when(2 * j != seq)
        def _():
            remote(
                obs.at[home], obs.at[home], obs_send_sem.at[j], obs_sem.at[home], 2 * j, seg
            ).start()

        return 0

    @pl.when(keeps)
    def _():
        for level in range(4):
            usable = (mask_ref[0, level] == 1) & (seq >= 2**level)
            row = jnp.full((8, 128), jnp.where(usable, 0.0, NEG), jnp.float32)
            bias[home, :, 128 * level : 128 * (level + 1)] = row
        lax.fori_loop(0, 16, send_bias, 0)
        own_obs.wait()

        @pl.when(seg >= 6)
        def _():
            lax.fori_loop(0, 8, send_obs, 0)

    row = lax.broadcasted_iota(jnp.int32, (256, 128), 0) % 128
    column = lax.broadcasted_iota(jnp.int32, (256, 128), 1)
    causal[...] = jnp.where(column <= row, 0.0, NEG)
    acc[...] = jnp.zeros_like(acc)

    @pl.when(lane == 0)
    def _():
        k_cross[0] = jnp.zeros_like(k_cross[0])
        v_cross[0] = jnp.zeros_like(v_cross[0])

    @pl.when(follows)
    def _():
        pl.semaphore_wait(token, 1)
        start_copy().start()

    @pl.when(leads)
    def _():
        start_copy().wait_send()
        signal(token, 2 * after + parity, after_seg)

    left = lax.broadcasted_iota(jnp.int32, (128, 128), 1) < 64

    def weight(t, i):
        @pl.when(t == 0)
        def _():
            target = weights[i][1]
            arrived(target, w_sem.at[i])

    def tick(t, _):
        @pl.when((seq + seg > 0) | (t > 0))
        def _():
            arrived(x_own.at[t], own_sem.at[t])

        weight(t, 0)
        normed[...] = rms(rows_of(x_own.at[t]).astype(jnp.float32), gain_ref[...])
        weight(t, 1)
        weight(t, 2)
        for c in range(CHUNKS):
            columns = slice(256 * c, 256 * (c + 1))
            k = jnp.dot(normed[...], wk[:, columns], preferred_element_type=jnp.float32)
            v = jnp.dot(normed[...], wv[:, columns], preferred_element_type=jnp.float32)
            for i in range(2):
                part = slice(128 * i, 128 * (i + 1))
                k_own[t, 2 * c + i] = k[:, part].astype(jnp.bfloat16)
                v_own[t, 2 * c + i] = v[:, part].astype(jnp.bfloat16)

        @pl.when(t + lane < TICKS)
        def _():
            for i, (mine, theirs) in enumerate(((k_own, k_cross), (v_own, v_cross))):
                remote(
                    mine.at[t],
                    theirs.at[t + lane],
                    send_cross_sem.at[i, t],
                    cross_sem.at[i, t + lane],
                    seq,
                    sibling,
                ).start()

        weight(t, 3)
        for c in range(CHUNKS):
            columns = slice(256 * c, 256 * (c + 1))
            q = jnp.dot(normed[...], wq[:, columns], preferred_element_type=jnp.float32) * 0.125
            for i in range(2):
                part = slice(128 * i, 128 * (i + 1))
                q_buf[2 * c + i, 0:128] = jnp.where(left, q[:, part], 0.0).astype(jnp.bfloat16)
                q_buf[2 * c + i, 128:256] = jnp.where(left, 0.0, q[:, part]).astype(jnp.bfloat16)

        @pl.when((t != home) | jnp.logical_not(keeps))
        def _():
            arrived(bias.at[t], bias_sem.at[t])

        @pl.when((lane == 1) | (t > 0))
        def _():
            arrived(k_cross.at[t], cross_sem.at[0, t])
            arrived(v_cross.at[t], cross_sem.at[1, t])

        def attend(p, levels):
            behind = [jnp.maximum(t - offset, 0) for offset in (1, 2, 4)[: levels - 1]]
            count = 128 * levels
            keys = jnp.concatenate(
                [k_own[t, p], k_cross[t, p]] + [k_own[index, p] for index in behind], axis=0
            )
            values = jnp.concatenate(
                [v_own[t, p], v_cross[t, p]] + [v_own[index, p] for index in behind], axis=0
            )
            ones = jnp.ones((128 + count, 128), jnp.bfloat16)
            scores = lax.dot_general(
                q_buf[p], keys, (((1,), (1,)), ((), ())), preferred_element_type=jnp.float32
            )
            scores = jnp.concatenate(
                [scores[:, 0:128] + causal[...], scores[:, 128:] + bias[t, 0:1, 0:count]], axis=1
            )
            peak = jnp.max(scores, axis=-1, keepdims=True)
            expon = jnp.exp(scores - peak).astype(jnp.bfloat16)
            both = jnp.dot(
                expon, jnp.concatenate([values, ones], axis=1), preferred_element_type=jnp.float32
            )
            mixed = both[:, 0:128] / both[:, 128:256]
            ctx[p] = jnp.where(left, mixed[0:128], mixed[128:256]).astype(jnp.bfloat16)

        def attend_all(levels):
            def some(i, _):
                for u in range(UNROLL):
                    attend(UNROLL * i + u, levels)
                return 0

            lax.fori_loop(0, PAIRS // UNROLL, some, 0)

        for levels, low_tick, high_tick in ((1, 0, 1), (2, 1, 2), (3, 2, 4), (4, 4, 8)):

            @pl.when((t >= low_tick) & (t < high_tick))
            def _():
                attend_all(levels)

        weight(t, 4)
        context = jnp.concatenate([ctx[p] for p in range(PAIRS)], axis=1)
        for c in range(CHUNKS):
            columns = slice(256 * c, 256 * (c + 1))
            mixed = jnp.dot(context, wo[:, columns], preferred_element_type=jnp.float32)
            x_out[t, c] = (x_own[t, c].astype(jnp.float32) + mixed).astype(jnp.bfloat16)

            @pl.when(stage < last)
            def _():
                remote(
                    x_out.at[t, c],
                    x_own.at[t, c],
                    send_own_sem.at[t],
                    own_sem.at[t],
                    next_seq,
                    next_seg,
                ).start()

        @pl.when(stage == last)
        def _():
            ended = rms(rows_of(x_out.at[t]).astype(jnp.float32), out_gain_ref[...])
            predicted = jnp.dot(ended, w_read_ref[...], preferred_element_type=jnp.float32)
            block = 2 * t + lane
            pred_send[t] = predicted

            @pl.when((block != seq) | (member != seg))
            def _():
                remote(
                    pred_send.at[t], pred_recv, pred_send_sem.at[t], pred_sem, block, member
                ).start()

            @pl.when((block == seq) & (member == seg))
            def _():
                pred_recv[...] = predicted

            @pl.when(block != seq)
            def _():
                arrived(obs.at[t], obs_sem.at[t])

            errors = predicted - obs[t]
            hours = lax.broadcasted_iota(jnp.int32, (128, 128), 0) + block * 128
            weighting = 1.0 + hours.astype(jnp.float32) * (2.0 / 2047.0)
            squares = weighting * errors * errors
            acc[...] += jnp.sum(squares.reshape(16, 8, 128), axis=0)

        return 0

    lax.fori_loop(0, TICKS, tick, 0)

    def fit_copy(j):
        return remote(
            fit_send, fit_recv.at[lane], fit_send_sem.at[j], fit_sem.at[lane], j, member
        )

    def send_fit(j, _):
        @pl.when((j != seq) | (member != seg))
        def _():
            fit_copy(j).start()

        return 0

    def sent_fit(j, _):
        @pl.when((j != seq) | (member != seg))
        def _():
            fit_copy(j).wait_send()

        return 0

    @pl.when(final)
    def _():
        fit_send[...] = acc[...]
        lax.fori_loop(0, 16, send_fit, 0)

        @pl.when(member == seg)
        def _():
            fit_recv[lane] = acc[...]

    def sent_tick(t, _):
        @pl.when(stage < last)
        def _():
            arrived(x_out.at[t], send_own_sem.at[t])

        @pl.when(t + lane < TICKS)
        def _():
            arrived(k_own.at[t], send_cross_sem.at[0, t])
            arrived(v_own.at[t], send_cross_sem.at[1, t])

        @pl.when(final & ((2 * t + lane != seq) | (member != seg)))
        def _():
            arrived(pred_send.at[t], pred_send_sem.at[t])

        @pl.when(keeps & (seg >= 6) & (2 * t != seq))
        def _():
            arrived(obs.at[home], obs_send_sem.at[t])

        return 0

    def sent_bias(j, _):
        @pl.when(j != seq)
        def _():
            arrived(bias.at[home], bias_send_sem.at[j])

        return 0

    lax.fori_loop(0, TICKS, sent_tick, 0)

    @pl.when(keeps)
    def _():
        lax.fori_loop(0, 16, sent_bias, 0)

    @pl.when((seq + seg > 0) & jnp.logical_not(leads))
    def _():
        start_copy().wait_send()

    @pl.when(owner)
    def _():
        for i, (source, target) in enumerate(weights):
            arrived(target, w_send_sem.at[i])

    @pl.when(final)
    def _():
        lax.fori_loop(0, 16, sent_fit, 0)

    @pl.when((seq != 2 * seg) | (seg != 6))
    def _():
        arrived(pred_recv, pred_sem)

    for source in range(2):

        @pl.when((seq != 2 * seg) | (seg != 6 + source))
        def _():
            arrived(fit_recv.at[source], fit_sem.at[source])

    pred_out[...] = pred_recv[...]
    total = jnp.sum(fit_recv[0] + fit_recv[1])
    fit_out[0] = -total / (2048.0 * 128.0)


def per_device(
    base_state,
    forcing,
    theta_base,
    perturb,
    order,
    w_force,
    attn_gain,
    w_query,
    w_key,
    w_value,
    w_out,
    block_mask,
    out_gain,
    w_read,
    observed,
):
    bf16, f32, i32 = jnp.bfloat16, jnp.float32, jnp.int32
    dma = pltpu.SemaphoreType.DMA
    predictions, fitness = pl.pallas_call(
        kernel,
        out_shape=(
            jax.ShapeDtypeStruct((128, 128), f32),
            jax.ShapeDtypeStruct((1,), f32),
        ),
        in_specs=[pl.BlockSpec(memory_space=pl.ANY)] * 15,
        out_specs=(
            pl.BlockSpec(memory_space=pltpu.VMEM),
            pl.BlockSpec(memory_space=pltpu.SMEM),
        ),
        scratch_shapes=[
            pltpu.VMEM((128, 1024), bf16),
            pltpu.VMEM((64, 128), f32),
            pltpu.VMEM((1, 64), f32),
            pltpu.VMEM((32, 64), f32),
            pltpu.SMEM((32,), i32),
            pltpu.VMEM((64, 1024), bf16),
            pltpu.VMEM((1, 1024), f32),
            pltpu.SMEM((1, 4), i32),
            pltpu.VMEM((1, 1024), f32),
            pltpu.VMEM((1024, 128), bf16),
            pltpu.VMEM((1024, 1024), bf16),
            pltpu.VMEM((1024, 1024), bf16),
            pltpu.VMEM((1024, 1024), bf16),
            pltpu.VMEM((1024, 1024), bf16),
            pltpu.VMEM((TICKS, CHUNKS, 128, 256), bf16),
            pltpu.VMEM((TICKS, CHUNKS, 128, 256), bf16),
            pltpu.VMEM((CHUNKS, 128, 256), bf16),
            pltpu.VMEM((128, 1024), bf16),
            pltpu.VMEM((PAIRS, 256, 128), bf16),
            pltpu.VMEM((TICKS, PAIRS, 128, 128), bf16),
            pltpu.VMEM((TICKS, PAIRS, 128, 128), bf16),
            pltpu.VMEM((TICKS, PAIRS, 128, 128), bf16),
            pltpu.VMEM((TICKS, PAIRS, 128, 128), bf16),
            pltpu.VMEM((PAIRS, 128, 128), bf16),
            pltpu.VMEM((256, 128), f32),
            pltpu.VMEM((TICKS, 8, 512), f32),
            pltpu.VMEM((TICKS, 128, 128), f32),
            pltpu.VMEM((TICKS, 128, 128), f32),
            pltpu.VMEM((128, 128), f32),
            pltpu.VMEM((8, 128), f32),
            pltpu.VMEM((8, 128), f32),
            pltpu.VMEM((2, 8, 128), f32),
            dma((10,)),
            dma((5,)),
            dma((5,)),
            dma((TICKS,)),
            dma((TICKS,)),
            dma((2, TICKS)),
            dma((2, TICKS)),
            dma,
            dma((TICKS,)),
            dma((16,)),
            dma((TICKS,)),
            dma((8,)),
            dma,
            dma((TICKS,)),
            dma((2,)),
            dma((16,)),
            pltpu.SemaphoreType.REGULAR,
        ],
        compiler_params=pltpu.CompilerParams(
            has_side_effects=True, collective_id=0, vmem_limit_bytes=60 * 1024 * 1024
        ),
    )(
        base_state,
        forcing.T,
        theta_base.reshape(1, -1),
        perturb,
        order,
        w_force,
        attn_gain,
        w_query,
        w_key,
        w_value,
        w_out,
        block_mask,
        out_gain.reshape(1, -1),
        w_read,
        observed,
    )
    return predictions[None], fitness


def solution(mesh):
    placed = (
        P("seq", None),
        P("seq", None),
        P(),
        P(),
        P(),
        P(),
        P("segment", None),
        P("segment", None, None),
        P("segment", None, None),
        P("segment", None, None),
        P("segment", None, None),
        P("seq", None),
        P(),
        P(),
        P("seq", None),
    )
    return jax.shard_map(
        per_device,
        mesh=mesh,
        in_specs=placed,
        out_specs=(P("segment", "seq", None), P("segment")),
        check_vma=False,
    )
```

time: 193 us -> 162 us (0.84)
  Pallas kernels: 178 us -> 157 us
  local copies, waits for them, and re-layouts: 12.4 us -> 1.47 us
    pallas_call x1, Pallas kernels: 178 us -> 157 us  [per_device(): pl.pallas_call(kernel, out_shape=(jax.ShapeDtypeStruct((128, 128), f32),...]
    unnamed x26 -> x1, local copies, waits for them, and re-layouts: 12.4 us -> 1.47 us
where the time goes in v2:
time: 162 us; the launch traced here: 161 us
  Pallas kernels  157 us (97%)
  between operations  2.39 us (1%)
    pallas_call x1, Pallas kernels, per_device(): pl.pallas_call(kernel, out_shape=(jax.ShapeDtypeStruct((128, 128), f32),...  157 us

profile of v2, /device:TPU:64, one launch (start us, length us, event | category | flops | bytes accessed | tf_op | source)
XLA Modules:
  0.0 161.3 jit_solution(1889666873304111512)
XLA Ops:
  0.6 157.5 %shard_map.158 = (f32[128,128]{1,0:T(8,128)}, f32[1]{0:T(128)}) custom-call(bf16[128,1024]{1,0:T(8,128)(2,1)} %base_hbm.1, f32[64,128]{1,0:T(8,128)} %bitcast.5, f32[1,64]{1,0:T(1,128)} %bitcast.7, f32[32,64]{1,0:T(8,128)} %perturb_hbm.1, s32[32]{0:T(128)} %order_hbm.1, bf16[64,1024]{1,0:T(8,128)(2,1)} %w_force_hbm.1, f32[1,1024]{1,0:T(1,128)} %gain_hbm.1, ...), custom_call_target="tpu_custom_call" | custom-call | tf_op jit(solution)/shard_map/pallas_call | solution.py:555
  158.1 1.5 copy.19

commit v3 on v1

--- a/solution.py
+++ b/solution.py
@@ -8,7 +8,7 @@
 TICKS = 8
 PAIRS = 8
 CHUNKS = 4
-AHEAD = 2
+UNROLL = 4
 NEG = -1e30
 
 
@@ -22,6 +22,23 @@
 
 
 def kernel(
+    base_hbm,
+    forcing_hbm,
+    theta_hbm,
+    perturb_hbm,
+    order_hbm,
+    w_force_hbm,
+    gain_hbm,
+    wq_hbm,
+    wk_hbm,
+    wv_hbm,
+    wo_hbm,
+    mask_hbm,
+    out_gain_hbm,
+    w_read_hbm,
+    observed_hbm,
+    pred_out,
+    fit_out,
     base_ref,
     forcing_ref,
     theta_ref,
@@ -29,16 +46,9 @@
     order_ref,
     w_force_ref,
     gain_ref,
-    wq_hbm,
-    wk_hbm,
-    wv_hbm,
-    wo_hbm,
     mask_ref,
     out_gain_ref,
     w_read_ref,
-    observed_ref,
-    pred_out,
-    fit_out,
     wq,
     wk,
     wv,
@@ -54,6 +64,8 @@
     k_cross,
     v_cross,
     ctx,
+    part,
+    peaks,
     causal,
     bias,
     obs,
@@ -76,6 +88,7 @@
     pred_send_sem,
     fit_sem,
     fit_send_sem,
+    token,
 ):
     seq = lax.axis_index("seq")
     seg = lax.axis_index("segment")
@@ -95,49 +108,122 @@
             device_id_type=pl.DeviceIdType.MESH,
         )
 
+    first = [
+        (base_hbm, base_ref),
+        (forcing_hbm, forcing_ref),
+        (theta_hbm, theta_ref),
+        (perturb_hbm, perturb_ref),
+        (order_hbm, order_ref),
+        (w_force_hbm, w_force_ref),
+    ]
+    second = [
+        (mask_hbm, mask_ref),
+        (gain_hbm, gain_ref),
+        (wq_hbm.at[0], wq),
+        (wk_hbm.at[0], wk),
+        (wv_hbm.at[0], wv),
+        (wo_hbm.at[0], wo),
+        (out_gain_hbm, out_gain_ref),
+        (w_read_hbm, w_read_ref),
+        (observed_hbm, obs.at[home]),
+    ]
+    def signal(sem, to_seq, to_seg):
+        pl.semaphore_signal(
+            sem,
+            inc=1,
+            device_id={"seq": to_seq, "segment": to_seg},
+            device_id_type=pl.DeviceIdType.MESH,
+        )
+
+    def arrived(ref, sem):
+        pltpu.make_async_copy(ref, ref, sem).wait()
+
     loads = [
-        pltpu.make_async_copy(hbm.at[0], vmem, w_sem.at[i])
-        for i, (hbm, vmem) in enumerate(((wq_hbm, wq), (wk_hbm, wk), (wv_hbm, wv), (wo_hbm, wo)))
+        pltpu.make_async_copy(source, target, w_sem.at[i])
+        for i, (source, target) in enumerate(first + second)
     ]
     for load in loads:
         load.start()
 
-    def send_start(m, _):
-        target = 2 * m + lane
-
-        @pl.when(target != seq)
-        def _():
-            remote(
-                starts.at[m], x_own.at[home], start_sem.at[m], own_sem.at[home], target, 0
-            ).start()
+    plane = seg // 2
+    core = seg % 2
+    slot = 2 * ((plane + 8 - home) % 4) + core
+    before = home - 3 + plane // 3
+    after = home + 3 - (plane % 2) * (1 - plane // 3)
+    follows = (plane > 0) & (before >= 0)
+    leads = (plane > 0) & (after < 8)
+
+    barrier = pltpu.get_barrier_semaphore()
+    even = 1 - seg % 2
+    ends = seg // last
+
+    @pl.when(seg > 0)
+    def _():
+        signal(barrier, seq, seg - 1)
+
+    signal(barrier, other, seg - seg % 2)
+
+    def greet(t, _):
+        source = 2 * t + lane
+
+        @pl.when(source != seq)
+        def _():
+            signal(barrier, source, seg)
+
+        @pl.when((seg == 0) & ((home > 0) | (t > 0)))
+        def _():
+            signal(barrier, source, 2 * ((member // 2 + t) % 4) + member % 2)
 
         return 0
 
-    def make_start(m, _):
-        theta = theta_ref[...] + 0.5 * perturb_ref[pl.ds(order_ref[m], 1), :]
-        drive = forcing_ref[...] * theta
-        high = drive.astype(jnp.bfloat16)
-        rest = drive - high.astype(jnp.float32)
-        middle = rest.astype(jnp.bfloat16)
-        low = (rest - middle.astype(jnp.float32)).astype(jnp.bfloat16)
-        for c in range(CHUNKS):
-            columns = slice(256 * c, 256 * (c + 1))
-            w = w_force_ref[:, columns]
-            lifted = jnp.dot(low, w, preferred_element_type=jnp.float32)
-            lifted += jnp.dot(middle, w, preferred_element_type=jnp.float32)
-            lifted += jnp.dot(high, w, preferred_element_type=jnp.float32)
-            starts[m, c] = (base_ref[:, columns].astype(jnp.float32) + lifted).astype(jnp.bfloat16)
-
-        @pl.when(home < AHEAD)
-        def _():
-            send_start(m, 0)
-
-        return 0
-
-    @pl.when(seg == 0)
-    def _():
-        lax.fori_loop(0, 8, make_start, 0)
-        x_own[home] = starts[member]
+    lax.fori_loop(0, TICKS, greet, 0)
+
+    @pl.when(follows)
+    def _():
+        signal(barrier, 2 * before + lane, 2 * (plane % 3 + 1) + core)
+
+    for source in range(2):
+
+        @pl.when((seq != 2 * seg + source) | (seg != last))
+        def _():
+            signal(barrier, 2 * seg + source, last)
+
+    expected = 9 - ends + 2 * even
+    expected += ((plane + 2) // 3) * (1 - after // 8)
+    expected += ends * (16 - member // last)
+    expected -= 1 - (seg + home + 13) // 14
+    pl.semaphore_wait(barrier, expected)
+
+    for load in loads[: len(first)]:
+        load.wait()
+
+    def start_copy():
+        return remote(starts, x_own.at[home], start_sem, own_sem.at[home, 0], 2 * slot + lane, 0)
+
+    theta = theta_ref[...] + 0.5 * perturb_ref[pl.ds(order_ref[slot], 1), :]
+    drive = forcing_ref[...].T * theta
+    high = drive.astype(jnp.bfloat16)
+    rest = drive - high.astype(jnp.float32)
+    middle = rest.astype(jnp.bfloat16)
+    low = (rest - middle.astype(jnp.float32)).astype(jnp.bfloat16)
+    for c in range(CHUNKS):
+        columns = slice(256 * c, 256 * (c + 1))
+        w = w_force_ref[:, columns]
+        lifted = jnp.dot(low, w, preferred_element_type=jnp.float32)
+        lifted += jnp.dot(middle, w, preferred_element_type=jnp.float32)
+        lifted += jnp.dot(high, w, preferred_element_type=jnp.float32)
+        starts[c] = (base_ref[:, columns].astype(jnp.float32) + lifted).astype(jnp.bfloat16)
+
+    @pl.when((seg == 0) & (home == 0))
+    def _():
+        x_own[0] = starts[...]
+
+    @pl.when((seg + home > 0) & jnp.logical_not(follows))
+    def _():
+        start_copy().start()
+
+    for load in loads[len(first) :]:
+        load.wait()
 
     for level in range(4):
         usable = (mask_ref[0, level] == 1) & (seq >= 2**level)
@@ -170,7 +256,6 @@
 
     @pl.when(seg == last)
     def _():
-        obs[home] = observed_ref[...]
         lax.fori_loop(0, 8, send_obs, 0)
 
     row = lax.broadcasted_iota(jnp.int32, (256, 128), 0) % 128
@@ -182,90 +267,117 @@
     def _():
         x_cross[0] = jnp.zeros_like(x_cross[0])
 
-    for load in loads:
-        load.wait()
-
     left = lax.broadcasted_iota(jnp.int32, (128, 128), 1) < 64
-    ones = jnp.ones((640, 128), jnp.bfloat16)
 
     def tick(t, _):
-        @pl.when((seg == 0) & (home >= AHEAD) & (t == home - AHEAD))
-        def _():
-            lax.fori_loop(0, 8, send_start, 0)
-
-        @pl.when((seg > 0) | (t != home))
-        def _():
-            pltpu.make_async_copy(x_own.at[t], x_own.at[t], own_sem.at[t]).wait()
-
-        @pl.when((seg == 0) & (t + lane < TICKS))
-        def _():
-            remote(
-                x_own.at[t],
-                x_cross.at[t + lane],
-                send_cross_sem.at[t],
-                cross_sem.at[t + lane],
-                other,
-                0,
-            ).start()
+        for c in range(CHUNKS):
+
+            @pl.when((seg == 0) & (t + home > 0) & (c == 0))
+            def _():
+                arrived(x_own.at[t], own_sem.at[t, 0])
+
+            @pl.when(seg > 0)
+            def _():
+                arrived(x_own.at[t, c], own_sem.at[t, c])
+
+            @pl.when((seg % 2 == 0) & (t + lane < TICKS))
+            def _():
+                remote(
+                    x_own.at[t, c],
+                    x_cross.at[t + lane, c],
+                    send_cross_sem.at[t],
+                    cross_sem.at[t + lane],
+                    other,
+                    seg,
+                ).start()
 
         x = rows_of(x_own.at[t]).astype(jnp.float32)
         gain = gain_ref[...]
         normed[0:128] = rms(x, gain)
 
-        @pl.when((lane == 1) | (t > 0))
-        def _():
-            pltpu.make_async_copy(x_cross.at[t], x_cross.at[t], cross_sem.at[t]).wait()
-
-        normed[128:256] = rms(rows_of(x_cross.at[t]).astype(jnp.float32), gain)
-
         for c in range(CHUNKS):
             columns = slice(256 * c, 256 * (c + 1))
             q = jnp.dot(normed[0:128], wq[:, columns], preferred_element_type=jnp.float32) * 0.125
-            k = jnp.dot(normed[...], wk[:, columns], preferred_element_type=jnp.float32)
-            v = jnp.dot(normed[...], wv[:, columns], preferred_element_type=jnp.float32)
+            k = jnp.dot(normed[0:128], wk[:, columns], preferred_element_type=jnp.float32)
+            v = jnp.dot(normed[0:128], wv[:, columns], preferred_element_type=jnp.float32)
             for i in range(2):
                 p = 2 * c + i
-                part = slice(128 * i, 128 * (i + 1))
-                q_buf[p, 0:128] = jnp.where(left, q[:, part], 0.0).astype(jnp.bfloat16)
-                q_buf[p, 128:256] = jnp.where(left, 0.0, q[:, part]).astype(jnp.bfloat16)
-                k_own[t, p] = k[0:128, part].astype(jnp.bfloat16)
-                k_cross[p] = k[128:256, part].astype(jnp.bfloat16)
-                v_own[t, p] = v[0:128, part].astype(jnp.bfloat16)
-                v_cross[p] = v[128:256, part].astype(jnp.bfloat16)
+                half = slice(128 * i, 128 * (i + 1))
+                q_buf[p, 0:128] = jnp.where(left, q[:, half], 0.0).astype(jnp.bfloat16)
+                q_buf[p, 128:256] = jnp.where(left, 0.0, q[:, half]).astype(jnp.bfloat16)
+                k_own[t, p] = k[:, half].astype(jnp.bfloat16)
+                v_own[t, p] = v[:, half].astype(jnp.bfloat16)
 
         @pl.when(t != home)
         def _():
-            pltpu.make_async_copy(bias.at[t], bias.at[t], bias_sem.at[t]).wait()
-
-        behind = [jnp.maximum(t - offset, 0) for offset in (1, 2, 4)]
-
-        def attend(p):
-            keys = jnp.concatenate(
-                [k_own[t, p], k_cross[p]] + [k_own[index, p] for index in behind], axis=0
-            )
-            values = jnp.concatenate(
-                [v_own[t, p], v_cross[p]] + [v_own[index, p] for index in behind], axis=0
-            )
-            scores = lax.dot_general(
+            arrived(bias.at[t], bias_sem.at[t])
+
+        def scores_of(p, keys):
+            return lax.dot_general(
                 q_buf[p], keys, (((1,), (1,)), ((), ())), preferred_element_type=jnp.float32
             )
-            scores = jnp.concatenate(
-                [scores[:, 0:128] + causal[...], scores[:, 128:640] + bias[t, 0:1, :]], axis=1
-            )
-            peak = jnp.max(scores, axis=-1, keepdims=True)
-            expon = jnp.exp(scores - peak).astype(jnp.bfloat16)
-            both = jnp.dot(
+
+        def mix(expon, values):
+            ones = jnp.ones((values.shape[0], 128), jnp.bfloat16)
+            return jnp.dot(
                 expon, jnp.concatenate([values, ones], axis=1), preferred_element_type=jnp.float32
             )
-            mixed = both[:, 0:128] / both[:, 128:256]
+
+        def all_pairs(unroll, attend):
+            def some(i, _):
+                for u in range(unroll):
+                    attend(unroll * i + u)
+                return 0
+
+            lax.fori_loop(0, PAIRS // unroll, some, 0)
+
+        def attend_own(p, levels):
+            behind = [t - offset for offset in (1, 2, 4)[: levels - 1]]
+            keys = jnp.concatenate([k_own[t, p]] + [k_own[index, p] for index in behind], axis=0)
+            values = jnp.concatenate([v_own[t, p]] + [v_own[index, p] for index in behind], axis=0)
+            scores = scores_of(p, keys)
+            seen = [scores[:, 0:128] + causal[...]]
+            if levels > 1:
+                seen.append(scores[:, 128:] + bias[t, 0:1, 128 : 128 * levels])
+            scores = jnp.concatenate(seen, axis=1)
+            peak = jnp.max(scores, axis=-1, keepdims=True)
+            part[p] = mix(jnp.exp(scores - peak).astype(jnp.bfloat16), values)
+            peaks[p] = jnp.broadcast_to(peak, (256, 128))
+
+        for levels, low_tick, high_tick in ((1, 0, 1), (2, 1, 2), (3, 2, 4), (4, 4, 8)):
+
+            @pl.when((t >= low_tick) & (t < high_tick))
+            def _():
+                all_pairs(UNROLL, lambda p: attend_own(p, levels))
+
+        @pl.when((lane == 1) | (t > 0))
+        def _():
+            arrived(x_cross.at[t], cross_sem.at[t])
+
+        normed[128:256] = rms(rows_of(x_cross.at[t]).astype(jnp.float32), gain)
+
+        for c in range(CHUNKS):
+            columns = slice(256 * c, 256 * (c + 1))
+            k = jnp.dot(normed[128:256], wk[:, columns], preferred_element_type=jnp.float32)
+            v = jnp.dot(normed[128:256], wv[:, columns], preferred_element_type=jnp.float32)
+            for i in range(2):
+                half = slice(128 * i, 128 * (i + 1))
+                k_cross[2 * c + i] = k[:, half].astype(jnp.bfloat16)
+                v_cross[2 * c + i] = v[:, half].astype(jnp.bfloat16)
+
+        def attend_cross(p):
+            scores = scores_of(p, k_cross[p]) + bias[t, 0:1, 0:128]
+            before = peaks[p]
+            peak = jnp.maximum(before, jnp.max(scores, axis=-1, keepdims=True))
+            scale = jnp.exp(before - peak)
+            added = mix(jnp.exp(scores - peak).astype(jnp.bfloat16), v_cross[p])
+            kept = part[p]
+            over = kept[:, 0:128] * scale + added[:, 0:128]
+            under = kept[:, 128:256] * scale + added[:, 128:256]
+            mixed = over / under
             ctx[p] = jnp.where(left, mixed[0:128], mixed[128:256]).astype(jnp.bfloat16)
 
-        def attend_two(i, _):
-            attend(2 * i)
-            attend(2 * i + 1)
-            return 0
-
-        lax.fori_loop(0, PAIRS // 2, attend_two, 0)
+        all_pairs(PAIRS, attend_cross)
 
         context = jnp.concatenate([ctx[p] for p in range(PAIRS)], axis=1)
         for c in range(CHUNKS):
@@ -276,10 +388,15 @@
             @pl.when(seg < last)
             def _():
                 remote(
-                    x_out.at[t, c], x_own.at[t, c], send_own_sem.at[t], own_sem.at[t], seq, seg + 1
+                    x_out.at[t, c],
+                    x_own.at[t, c],
+                    send_own_sem.at[t],
+                    own_sem.at[t, c],
+                    seq,
+                    seg + 1,
                 ).start()
 
-            @pl.when((seg < last) & (t + lane < TICKS))
+            @pl.when((seg % 2 == 0) & (t + lane < TICKS))
             def _():
                 remote(
                     x_out.at[t, c],
@@ -319,6 +436,16 @@
 
         return 0
 
+    @pl.when(follows)
+    def _():
+        pl.semaphore_wait(token, 1)
+        start_copy().start()
+
+    @pl.when(leads)
+    def _():
+        start_copy().wait_send()
+        signal(token, 2 * after + lane, 2 * ((plane + 1) % 3 + 1) + core)
+
     lax.fori_loop(0, TICKS, tick, 0)
 
     def send_fit(j, _):
@@ -353,18 +480,11 @@
         def _():
             pltpu.make_async_copy(x_out.at[t], x_out.at[t], send_own_sem.at[t]).wait()
 
-            @pl.when(t + lane < TICKS)
-            def _():
-                pltpu.make_async_copy(x_out.at[t], x_out.at[t], send_cross_sem.at[t + TICKS]).wait()
-
-        @pl.when((seg == 0) & (t + lane < TICKS))
-        def _():
+        @pl.when((seg % 2 == 0) & (t + lane < TICKS))
+        def _():
+            pltpu.make_async_copy(x_out.at[t], x_out.at[t], send_cross_sem.at[t + TICKS]).wait()
             pltpu.make_async_copy(x_own.at[t], x_own.at[t], send_cross_sem.at[t]).wait()
 
-        @pl.when((seg == 0) & (2 * t + lane != seq))
-        def _():
-            pltpu.make_async_copy(starts.at[t], starts.at[t], start_sem.at[t]).wait()
-
         @pl.when(2 * t + lane != seq)
         def _():
             pltpu.make_async_copy(bias.at[home], bias.at[home], bias_send_sem.at[t]).wait()
@@ -382,6 +502,10 @@
         return 0
 
     lax.fori_loop(0, TICKS, sent_tick, 0)
+
+    @pl.when((seg + home > 0) & jnp.logical_not(leads))
+    def _():
+        start_copy().wait_send()
 
     @pl.when(seg == last)
     def _():
@@ -430,9 +554,19 @@
             jax.ShapeDtypeStruct((128, 128), f32),
             jax.ShapeDtypeStruct((1,), f32),
         ),
-        in_specs=[vmem, vmem, vmem, vmem, smem, vmem, vmem, hbm, hbm, hbm, hbm, smem, vmem, vmem, vmem],
+        in_specs=[hbm] * 15,
         out_specs=(vmem, smem),
         scratch_shapes=[
+            pltpu.VMEM((128, 1024), bf16),
+            pltpu.VMEM((64, 128), f32),
+            pltpu.VMEM((1, 64), f32),
+            pltpu.VMEM((32, 64), f32),
+            pltpu.SMEM((32,), jnp.int32),
+            pltpu.VMEM((64, 1024), bf16),
+            pltpu.VMEM((1, 1024), f32),
+            pltpu.SMEM((1, 4), jnp.int32),
+            pltpu.VMEM((1, 1024), f32),
+            pltpu.VMEM((1024, 128), bf16),
             pltpu.VMEM((1024, 1024), bf16),
             pltpu.VMEM((1024, 1024), bf16),
             pltpu.VMEM((1024, 1024), bf16),
@@ -440,7 +574,7 @@
             pltpu.VMEM((TICKS, CHUNKS, 128, 256), bf16),
             pltpu.VMEM((TICKS, CHUNKS, 128, 256), bf16),
             pltpu.VMEM((TICKS, CHUNKS, 128, 256), bf16),
-            pltpu.VMEM((8, CHUNKS, 128, 256), bf16),
+            pltpu.VMEM((CHUNKS, 128, 256), bf16),
             pltpu.VMEM((256, 1024), bf16),
             pltpu.VMEM((PAIRS, 256, 128), bf16),
             pltpu.VMEM((TICKS, PAIRS, 128, 128), bf16),
@@ -448,6 +582,8 @@
             pltpu.VMEM((PAIRS, 128, 128), bf16),
             pltpu.VMEM((PAIRS, 128, 128), bf16),
             pltpu.VMEM((PAIRS, 128, 128), bf16),
+            pltpu.VMEM((PAIRS, 256, 256), f32),
+            pltpu.VMEM((PAIRS, 256, 128), f32),
             pltpu.VMEM((256, 128), f32),
             pltpu.VMEM((TICKS, 8, 512), f32),
             pltpu.VMEM((TICKS, 128, 128), f32),
@@ -456,12 +592,12 @@
             pltpu.VMEM((8, 128), f32),
             pltpu.VMEM((8, 128), f32),
             pltpu.VMEM((2, 8, 128), f32),
-            dma((4,)),
-            dma((TICKS,)),
+            dma((15,)),
+            dma((TICKS, CHUNKS)),
             dma((TICKS,)),
             dma((TICKS,)),
             dma((2 * TICKS,)),
-            dma((8,)),
+            dma,
             dma((TICKS,)),
             dma((8,)),
             dma((TICKS,)),
@@ -470,13 +606,14 @@
             dma((TICKS,)),
             dma((2,)),
             dma((16,)),
+            pltpu.SemaphoreType.REGULAR,
         ],
         compiler_params=pltpu.CompilerParams(
-            has_side_effects=True, vmem_limit_bytes=48 * 1024 * 1024
+            has_side_effects=True, collective_id=0, vmem_limit_bytes=60 * 1024 * 1024
         ),
     )(
         base_state,
-        forcing,
+        forcing.T,
         theta_base.reshape(1, -1),
         perturb,
         order,

time: 193 us -> 147 us (0.76)
  Pallas kernels: 178 us -> 142 us
  local copies, waits for them, and re-layouts: 12.4 us -> 1.47 us
    pallas_call x1, Pallas kernels: 178 us -> 142 us  [per_device(): pl.pallas_call(kernel, out_shape=(jax.ShapeDtypeStruct((128, 128), f32),...]
    unnamed x26 -> x1, local copies, waits for them, and re-layouts: 12.4 us -> 1.47 us
where the time goes in v3:
time: 147 us; the launch traced here: 146 us
  Pallas kernels  142 us (97%)
  between operations  2.39 us (2%)
  local copies, waits for them, and re-layouts  1.47 us (1%)
    pallas_call x1, Pallas kernels, per_device(): pl.pallas_call(kernel, out_shape=(jax.ShapeDtypeStruct((128, 128), f32),...  142 us

profile of v3, /device:TPU:64, one launch (start us, length us, event | category | flops | bytes accessed | tf_op | source)
XLA Modules:
  0.0 146.0 jit_solution(7129349166848339327)
XLA Ops:
  0.6 142.1 %shard_map.158 = (f32[128,128]{1,0:T(8,128)}, f32[1]{0:T(128)}) custom-call(bf16[128,1024]{1,0:T(8,128)(2,1)} %base_hbm.1, f32[64,128]{1,0:T(8,128)} %bitcast.5, f32[1,64]{1,0:T(1,128)} %bitcast.7, f32[32,64]{1,0:T(8,128)} %perturb_hbm.1, s32[32]{0:T(128)} %order_hbm.1, bf16[64,1024]{1,0:T(8,128)(2,1)} %w_force_hbm.1, f32[1,1024]{1,0:T(1,128)} %gain_hbm.1, ...), custom_call_target="tpu_custom_call" | custom-call | tf_op jit(solution)/shard_map/pallas_call | solution.py:551
  142.7 1.5 %copy.19 = f32[1,128,128]{2,1,0:T(8,128)} copy(f32[1,128,128]{2,1,0:T(8,128)} %bitcast.4) | data formatting | bytes 131072

commit v4 on v3

--- a/solution.py
+++ b/solution.py
@@ -8,7 +8,6 @@
 TICKS = 8
 PAIRS = 8
 CHUNKS = 4
-UNROLL = 4
 NEG = -1e30
 
 
@@ -154,14 +153,13 @@
     leads = (plane > 0) & (after < 8)
 
     barrier = pltpu.get_barrier_semaphore()
-    even = 1 - seg % 2
     ends = seg // last
 
     @pl.when(seg > 0)
     def _():
         signal(barrier, seq, seg - 1)
 
-    signal(barrier, other, seg - seg % 2)
+    signal(barrier, other, seg)
 
     def greet(t, _):
         source = 2 * t + lane
@@ -188,12 +186,10 @@
         def _():
             signal(barrier, 2 * seg + source, last)
 
-    expected = 9 - ends + 2 * even
+    expected = 10 - ends
     expected += ((plane + 2) // 3) * (1 - after // 8)
     expected += ends * (16 - member // last)
     expected -= 1 - (seg + home + 13) // 14
-    pl.semaphore_wait(barrier, expected)
-
     for load in loads[: len(first)]:
         load.wait()
 
@@ -218,6 +214,8 @@
     def _():
         x_own[0] = starts[...]
 
+    pl.semaphore_wait(barrier, expected)
+
     @pl.when((seg + home > 0) & jnp.logical_not(follows))
     def _():
         start_copy().start()
@@ -280,7 +278,7 @@
             def _():
                 arrived(x_own.at[t, c], own_sem.at[t, c])
 
-            @pl.when((seg % 2 == 0) & (t + lane < TICKS))
+            @pl.when(t + lane < TICKS)
             def _():
                 remote(
                     x_own.at[t, c],
@@ -291,26 +289,11 @@
                     seg,
                 ).start()
 
-        x = rows_of(x_own.at[t]).astype(jnp.float32)
+        @pl.when(t != home)
+        def _():
+            arrived(bias.at[t], bias_sem.at[t])
+
         gain = gain_ref[...]
-        normed[0:128] = rms(x, gain)
-
-        for c in range(CHUNKS):
-            columns = slice(256 * c, 256 * (c + 1))
-            q = jnp.dot(normed[0:128], wq[:, columns], preferred_element_type=jnp.float32) * 0.125
-            k = jnp.dot(normed[0:128], wk[:, columns], preferred_element_type=jnp.float32)
-            v = jnp.dot(normed[0:128], wv[:, columns], preferred_element_type=jnp.float32)
-            for i in range(2):
-                p = 2 * c + i
-                half = slice(128 * i, 128 * (i + 1))
-                q_buf[p, 0:128] = jnp.where(left, q[:, half], 0.0).astype(jnp.bfloat16)
-                q_buf[p, 128:256] = jnp.where(left, 0.0, q[:, half]).astype(jnp.bfloat16)
-                k_own[t, p] = k[:, half].astype(jnp.bfloat16)
-                v_own[t, p] = v[:, half].astype(jnp.bfloat16)
-
-        @pl.when(t != home)
-        def _():
-            arrived(bias.at[t], bias_sem.at[t])
 
         def scores_of(p, keys):
             return lax.dot_general(
@@ -323,39 +306,57 @@
                 expon, jnp.concatenate([values, ones], axis=1), preferred_element_type=jnp.float32
             )
 
-        def all_pairs(unroll, attend):
-            def some(i, _):
-                for u in range(unroll):
-                    attend(unroll * i + u)
-                return 0
-
-            lax.fori_loop(0, PAIRS // unroll, some, 0)
-
-        def attend_own(p, levels):
-            behind = [t - offset for offset in (1, 2, 4)[: levels - 1]]
-            keys = jnp.concatenate([k_own[t, p]] + [k_own[index, p] for index in behind], axis=0)
-            values = jnp.concatenate([v_own[t, p]] + [v_own[index, p] for index in behind], axis=0)
-            scores = scores_of(p, keys)
-            seen = [scores[:, 0:128] + causal[...]]
-            if levels > 1:
-                seen.append(scores[:, 128:] + bias[t, 0:1, 128 : 128 * levels])
-            scores = jnp.concatenate(seen, axis=1)
-            peak = jnp.max(scores, axis=-1, keepdims=True)
-            part[p] = mix(jnp.exp(scores - peak).astype(jnp.bfloat16), values)
-            peaks[p] = jnp.broadcast_to(peak, (256, 128))
-
-        for levels, low_tick, high_tick in ((1, 0, 1), (2, 1, 2), (3, 2, 4), (4, 4, 8)):
-
-            @pl.when((t >= low_tick) & (t < high_tick))
-            def _():
-                all_pairs(UNROLL, lambda p: attend_own(p, levels))
+        def both(pair):
+            return jnp.where(left, pair[0:128], pair[128:256])
+
+        def own_part(levels):
+            normed[0:128] = rms(rows_of(x_own.at[t]).astype(jnp.float32), gain)
+            for c in range(CHUNKS):
+                columns = slice(256 * c, 256 * (c + 1))
+                mine = normed[0:128]
+                q = jnp.dot(mine, wq[:, columns], preferred_element_type=jnp.float32) * 0.125
+                k = jnp.dot(mine, wk[:, columns], preferred_element_type=jnp.float32)
+                v = jnp.dot(mine, wv[:, columns], preferred_element_type=jnp.float32)
+                for i in range(2):
+                    p = 2 * c + i
+                    half = slice(128 * i, 128 * (i + 1))
+                    q_buf[p, 0:128] = jnp.where(left, q[:, half], 0.0).astype(jnp.bfloat16)
+                    q_buf[p, 128:256] = jnp.where(left, 0.0, q[:, half]).astype(jnp.bfloat16)
+                    k_own[t, p] = k[:, half].astype(jnp.bfloat16)
+                    v_own[t, p] = v[:, half].astype(jnp.bfloat16)
+            behind = [jnp.maximum(t - offset, 0) for offset in (1, 2, 4)[: levels - 1]]
+            for p in range(PAIRS):
+                keys = jnp.concatenate([k_own[t, p]] + [k_own[index, p] for index in behind], axis=0)
+                values = jnp.concatenate(
+                    [v_own[t, p]] + [v_own[index, p] for index in behind], axis=0
+                )
+                scores = scores_of(p, keys)
+                scores = jnp.concatenate(
+                    [
+                        scores[:, 0:128] + causal[...],
+                        scores[:, 128:] + bias[t, 0:1, 128 : 128 * levels],
+                    ],
+                    axis=1,
+                )
+                peak = jnp.max(scores, axis=-1, keepdims=True)
+                mixed = mix(jnp.exp(scores - peak).astype(jnp.bfloat16), values)
+                part[p, :, 0:128] = both(mixed[:, 0:128])
+                part[p, :, 128:256] = both(mixed[:, 128:256])
+                peaks[p] = jnp.broadcast_to(peak, (256, 128))
+
+        @pl.when(t < 2)
+        def _():
+            own_part(2)
+
+        @pl.when(t >= 2)
+        def _():
+            own_part(4)
 
         @pl.when((lane == 1) | (t > 0))
         def _():
             arrived(x_cross.at[t], cross_sem.at[t])
 
         normed[128:256] = rms(rows_of(x_cross.at[t]).astype(jnp.float32), gain)
-
         for c in range(CHUNKS):
             columns = slice(256 * c, 256 * (c + 1))
             k = jnp.dot(normed[128:256], wk[:, columns], preferred_element_type=jnp.float32)
@@ -364,29 +365,24 @@
                 half = slice(128 * i, 128 * (i + 1))
                 k_cross[2 * c + i] = k[:, half].astype(jnp.bfloat16)
                 v_cross[2 * c + i] = v[:, half].astype(jnp.bfloat16)
-
-        def attend_cross(p):
+        for p in range(PAIRS):
             scores = scores_of(p, k_cross[p]) + bias[t, 0:1, 0:128]
-            before = peaks[p]
-            peak = jnp.maximum(before, jnp.max(scores, axis=-1, keepdims=True))
-            scale = jnp.exp(before - peak)
+            earlier = peaks[p]
+            peak = jnp.maximum(earlier, jnp.max(scores, axis=-1, keepdims=True))
+            scale = jnp.exp(both(earlier - peak))
             added = mix(jnp.exp(scores - peak).astype(jnp.bfloat16), v_cross[p])
-            kept = part[p]
-            over = kept[:, 0:128] * scale + added[:, 0:128]
-            under = kept[:, 128:256] * scale + added[:, 128:256]
-            mixed = over / under
-            ctx[p] = jnp.where(left, mixed[0:128], mixed[128:256]).astype(jnp.bfloat16)
-
-        all_pairs(PAIRS, attend_cross)
-
+            over = part[p, :, 0:128] * scale + both(added[:, 0:128])
+            under = part[p, :, 128:256] * scale + both(added[:, 128:256])
+            ctx[p] = (over / under).astype(jnp.bfloat16)
         context = jnp.concatenate([ctx[p] for p in range(PAIRS)], axis=1)
         for c in range(CHUNKS):
             columns = slice(256 * c, 256 * (c + 1))
             mixed = jnp.dot(context, wo[:, columns], preferred_element_type=jnp.float32)
             x_out[t, c] = (x_own[t, c].astype(jnp.float32) + mixed).astype(jnp.bfloat16)
 
-            @pl.when(seg < last)
-            def _():
+        @pl.when(seg < last)
+        def _():
+            for c in range(CHUNKS):
                 remote(
                     x_out.at[t, c],
                     x_own.at[t, c],
@@ -396,17 +392,6 @@
                     seg + 1,
                 ).start()
 
-            @pl.when((seg % 2 == 0) & (t + lane < TICKS))
-            def _():
-                remote(
-                    x_out.at[t, c],
-                    x_cross.at[t + lane, c],
-                    send_cross_sem.at[t + TICKS],
-                    cross_sem.at[t + lane],
-                    other,
-                    seg + 1,
-                ).start()
-
         @pl.when(seg == last)
         def _():
             final = rms(rows_of(x_out.at[t]).astype(jnp.float32), out_gain_ref[...])
@@ -480,9 +465,8 @@
         def _():
             pltpu.make_async_copy(x_out.at[t], x_out.at[t], send_own_sem.at[t]).wait()
 
-        @pl.when((seg % 2 == 0) & (t + lane < TICKS))
-        def _():
-            pltpu.make_async_copy(x_out.at[t], x_out.at[t], send_cross_sem.at[t + TICKS]).wait()
+        @pl.when(t + lane < TICKS)
+        def _():
             pltpu.make_async_copy(x_own.at[t], x_own.at[t], send_cross_sem.at[t]).wait()
 
         @pl.when(2 * t + lane != seq)
@@ -582,7 +566,7 @@
             pltpu.VMEM((PAIRS, 128, 128), bf16),
             pltpu.VMEM((PAIRS, 128, 128), bf16),
             pltpu.VMEM((PAIRS, 128, 128), bf16),
-            pltpu.VMEM((PAIRS, 256, 256), f32),
+            pltpu.VMEM((PAIRS, 128, 256), f32),
             pltpu.VMEM((PAIRS, 256, 128), f32),
             pltpu.VMEM((256, 128), f32),
             pltpu.VMEM((TICKS, 8, 512), f32),
@@ -596,7 +580,7 @@
             dma((TICKS, CHUNKS)),
             dma((TICKS,)),
             dma((TICKS,)),
-            dma((2 * TICKS,)),
+            dma((TICKS,)),
             dma,
             dma((TICKS,)),
             dma((8,)),

time: 147 us -> 140 us (0.952)
  Pallas kernels: 142 us -> 135 us
    pallas_call x1, Pallas kernels: 142 us -> 135 us  [per_device(): pl.pallas_call(kernel, out_shape=(jax.ShapeDtypeStruct((128, 128), f32),...]
where the time goes in v4:
time: 140 us; the launch traced here: 139 us
  Pallas kernels  135 us (96%)
  between operations  2.39 us (2%)
  local copies, waits for them, and re-layouts  1.47 us (1%)
    pallas_call x1, Pallas kernels, per_device(): pl.pallas_call(kernel, out_shape=(jax.ShapeDtypeStruct((128, 128), f32),...  135 us

profile of v4, /device:TPU:64, one launch (start us, length us, event | category | flops | bytes accessed | tf_op | source)
XLA Modules:
  0.0 139.4 jit_solution(1391205429063313128)
XLA Ops:
  0.6 135.5 %shard_map.158 = (f32[128,128]{1,0:T(8,128)}, f32[1]{0:T(128)}) custom-call(bf16[128,1024]{1,0:T(8,128)(2,1)} %base_hbm.1, f32[64,128]{1,0:T(8,128)} %bitcast.5, f32[1,64]{1,0:T(1,128)} %bitcast.7, f32[32,64]{1,0:T(8,128)} %perturb_hbm.1, s32[32]{0:T(128)} %order_hbm.1, bf16[64,1024]{1,0:T(8,128)(2,1)} %w_force_hbm.1, f32[1,1024]{1,0:T(1,128)} %gain_hbm.1, ...), custom_call_target="tpu_custom_call" | custom-call | tf_op jit(solution)/shard_map/pallas_call | solution.py:535
  136.1 1.5 %copy.19 = f32[1,128,128]{2,1,0:T(8,128)} copy(f32[1,128,128]{2,1,0:T(8,128)} %bitcast.4) | data formatting | bytes 131072

commit v5 on v4

--- a/solution.py
+++ b/solution.py
@@ -141,7 +141,7 @@
         pltpu.make_async_copy(source, target, w_sem.at[i])
         for i, (source, target) in enumerate(first + second)
     ]
-    for load in loads:
+    for load in loads[: len(first)]:
         load.start()
 
     plane = seg // 2
@@ -192,6 +192,8 @@
     expected -= 1 - (seg + home + 13) // 14
     for load in loads[: len(first)]:
         load.wait()
+    for load in loads[len(first) :]:
+        load.start()
 
     def start_copy():
         return remote(starts, x_own.at[home], start_sem, own_sem.at[home, 0], 2 * slot + lane, 0)
@@ -202,6 +204,8 @@
     rest = drive - high.astype(jnp.float32)
     middle = rest.astype(jnp.bfloat16)
     low = (rest - middle.astype(jnp.float32)).astype(jnp.bfloat16)
+    pl.semaphore_wait(barrier, expected)
+
     for c in range(CHUNKS):
         columns = slice(256 * c, 256 * (c + 1))
         w = w_force_ref[:, columns]
@@ -210,15 +214,16 @@
         lifted += jnp.dot(high, w, preferred_element_type=jnp.float32)
         starts[c] = (base_ref[:, columns].astype(jnp.float32) + lifted).astype(jnp.bfloat16)
 
+        @pl.when((seg + home > 0) & jnp.logical_not(follows))
+        def _():
+            remote(
+                starts.at[c], x_own.at[home, c], start_sem, own_sem.at[home, 0], 2 * slot + lane, 0
+            ).start()
+
     @pl.when((seg == 0) & (home == 0))
     def _():
         x_own[0] = starts[...]
 
-    pl.semaphore_wait(barrier, expected)
-
-    @pl.when((seg + home > 0) & jnp.logical_not(follows))
-    def _():
-        start_copy().start()
 
     for load in loads[len(first) :]:
         load.wait()
@@ -268,26 +273,35 @@
     left = lax.broadcasted_iota(jnp.int32, (128, 128), 1) < 64
 
     def tick(t, _):
-        for c in range(CHUNKS):
-
-            @pl.when((seg == 0) & (t + home > 0) & (c == 0))
-            def _():
-                arrived(x_own.at[t], own_sem.at[t, 0])
-
-            @pl.when(seg > 0)
-            def _():
+        def hand_on(c):
+            remote(
+                x_own.at[t, c],
+                x_cross.at[t + lane, c],
+                send_cross_sem.at[t],
+                cross_sem.at[t + lane],
+                other,
+                seg,
+            ).start()
+
+        @pl.when((seg == 0) & (t + home > 0))
+        def _():
+            arrived(x_own.at[t], own_sem.at[t, 0])
+
+        @pl.when((seg == 0) & (t + lane < TICKS))
+        def _():
+            for c in range(CHUNKS):
+                hand_on(c)
+
+        @pl.when((seg > 0) & (t + lane < TICKS))
+        def _():
+            for c in range(CHUNKS):
                 arrived(x_own.at[t, c], own_sem.at[t, c])
-
-            @pl.when(t + lane < TICKS)
-            def _():
-                remote(
-                    x_own.at[t, c],
-                    x_cross.at[t + lane, c],
-                    send_cross_sem.at[t],
-                    cross_sem.at[t + lane],
-                    other,
-                    seg,
-                ).start()
+                hand_on(c)
+
+        @pl.when((seg > 0) & (t + lane >= TICKS))
+        def _():
+            for c in range(CHUNKS):
+                arrived(x_own.at[t, c], own_sem.at[t, c])
 
         @pl.when(t != home)
         def _():

time: 140 us -> 141 us (level)
  no operation moved by 1% of the time
where the time goes in v5:
time: 141 us; the launch traced here: 140 us
  Pallas kernels  136 us (96%)
  between operations  2.39 us (2%)
  local copies, waits for them, and re-layouts  1.47 us (1%)
    pallas_call x1, Pallas kernels, per_device(): pl.pallas_call(kernel, out_shape=(jax.ShapeDtypeStruct((128, 128), f32),...  136 us

profile of v5, /device:TPU:64, one launch (start us, length us, event | category | flops | bytes accessed | tf_op | source)
XLA Modules:
  0.0 139.9 jit_solution(424654975855897380)
XLA Ops:
  0.6 136.0 %shard_map.158 = (f32[128,128]{1,0:T(8,128)}, f32[1]{0:T(128)}) custom-call(bf16[128,1024]{1,0:T(8,128)(2,1)} %base_hbm.1, f32[64,128]{1,0:T(8,128)} %bitcast.5, f32[1,64]{1,0:T(1,128)} %bitcast.7, f32[32,64]{1,0:T(8,128)} %perturb_hbm.1, s32[32]{0:T(128)} %order_hbm.1, bf16[64,1024]{1,0:T(8,128)(2,1)} %w_force_hbm.1, f32[1,1024]{1,0:T(1,128)} %gain_hbm.1, ...), custom_call_target="tpu_custom_call" | custom-call | tf_op jit(solution)/shard_map/pallas_call | solution.py:549
  136.6 1.5 %copy.19 = f32[1,128,128]{2,1,0:T(8,128)} copy(f32[1,128,128]{2,1,0:T(8,128)} %bitcast.4) | data formatting | bytes 131072
